TPU v7x, 128 devices: a whole 4x4x4 slice. The times are simulated.
128 devices in a mesh: shard: 8 (over y_lo, z), ctx: 8 (over y_hi, x), tp: 2 (over core).
Axes of the slice: x: 4, y: 4 (y_hi: 2, y_lo: 2; y = y_hi * 2 + y_lo), z: 4, core: 2. Of those that a mesh axis runs over, the one named last changes fastest.
Arguments:
- tokens: bfloat16 [8, 2048, 2048], P('shard', 'ctx'), may hold values from -6 to 6
- cotangent: bfloat16 [8, 2048, 2048], P('shard', 'ctx'), may hold values from -6 to 6
- seq_ids: int32 [8, 2048], P('shard'), may hold values from 0 to 1, as said below
- block_ids: int32 [8, 2048], P('shard'), may hold values from 0 to 7, as said below
- keep_layer: int32 [8], P('shard'), may hold values from 0 to 1, as said below
- gain_attn: float32 [2048], replicated, may hold values from 0.25 to 1.75
- gain_ffn: float32 [2048], replicated, may hold values from 0.25 to 1.75
- w_query: float32 [2048, 2048], P('shard', 'tp'), may hold values from -0.125 to 0.125
- w_key: float32 [2048, 512], P('shard', 'tp'), may hold values from -0.125 to 0.125
- w_value: float32 [2048, 512], P('shard', 'tp'), may hold values from -0.125 to 0.125
- w_out: float32 [2048, 2048], P('shard', 'tp'), may hold values from -0.75 to 0.75
- w_gate: float32 [2048, 5632], P('shard', 'tp'), may hold values from -0.125 to 0.125
- w_up: float32 [2048, 5632], P('shard', 'tp'), may hold values from -0.125 to 0.125
- w_down: float32 [2048, 5632], P('shard', 'tp'), may hold values from -0.078125 to 0.078125
Outputs:
- output: bfloat16 [8, 2048, 2048], P('shard', 'ctx')
- input_grad: bfloat16 [8, 2048, 2048], P('shard', 'ctx')
- grad_gain_attn: float32 [2048], P('shard')
- grad_gain_ffn: float32 [2048], P('shard')
- grad_query: float32 [2048, 2048], P('shard', 'tp')
- grad_key: float32 [2048, 512], P('shard', 'tp')
- grad_value: float32 [2048, 512], P('shard', 'tp')
- grad_out: float32 [2048, 2048], P('shard', 'tp')
- grad_gate: float32 [2048, 5632], P('shard', 'tp')
- grad_up: float32 [2048, 5632], P('shard', 'tp')
- grad_down: float32 [2048, 5632], P('shard', 'tp')
Inputs may be any that keep to these rules, and one draw needn't show every extreme that they name: `seq_ids`: each sample holds exactly two documents: id 0 on a leading run of fewer than min(256, 256) positions, id 1 on the rest. Blocks of 256 positions are counted from each document's start: block_ids[p] = (p - start of p's document) // 256. `keep_layer`: at least one sample runs the layer and at least one skips it.
All inputs are finite; a program needn't handle non-finite values.
Results may differ from a plain program's by a relative error of at most 0.02.
Values may be sent and summed in bfloat16 or wider, within the bound.
No kernel may reach another device: no remote copies, remote signals or barrier semaphores. Data moves between devices by JAX's collectives and lax.ppermute only.
A program may use at most 256 MiB of HBM per device.

v0:
```python
import jax
import jax.numpy as jnp
from jax import lax
from jax.sharding import Mesh, PartitionSpec as P

HD = 128
EPS = 1e-05
NEG = -1e30
F32 = jnp.float32
BF16 = jnp.bfloat16
SHARD = ("yl", "z")
SWAP = ((0, 1), (1, 0))


def half(value):
    return value.astype(BF16)


def mm(left, right):
    return jnp.dot(left, right, preferred_element_type=F32)


def mm_nt(left, right):
    return lax.dot_general(left, right, (((1,), (1,)), ((), ())), preferred_element_type=F32)


def mm_tn(left, right):
    return lax.dot_general(left, right, (((0,), (0,)), ((), ())), preferred_element_type=F32)


def swap_cores(value):
    return lax.ppermute(value, "tp", SWAP)


def shift_x(value, hop):
    return lax.ppermute(value, "x", [(i, (i + hop) % 4) for i in range(4)])


def gather_x(value):
    return [value] + [shift_x(value, -hop) for hop in (1, 2, 3)]


def scatter_x(chunks):
    moved = [shift_x(half(chunks[hop]), hop) for hop in (2, 1, 3)]
    return chunks[0] + moved[0].astype(F32) + moved[1].astype(F32) + moved[2].astype(F32)


def absolute(chunks, x_at):
    stacked = jnp.stack(chunks + chunks[:3])
    return lax.dynamic_slice_in_dim(stacked, (4 - x_at) % 4, 4, axis=0)


def rotate(value, cosine, sine):
    turned = jnp.concatenate([-value[..., HD // 2 :], value[..., : HD // 2]], axis=-1)
    return value * cosine + turned * sine


def unrotate(grad, cosine, sine):
    scaled = grad * sine
    return grad * cosine + jnp.concatenate(
        [scaled[..., HD // 2 :], -scaled[..., : HD // 2]], axis=-1
    )


def norm_root(value):
    return lax.rsqrt(jnp.mean(value * value, axis=-1, keepdims=True) + EPS)


def norm_backward(value, root, gain, grad):
    scaled = gain * grad
    grad_value = root * scaled - value * root**3 * jnp.mean(scaled * value, axis=-1, keepdims=True)
    return (grad_value, jnp.sum(grad * value * root, axis=0))


def per_device(
    tokens,
    cotangent,
    seq_ids,
    block_ids,
    keep_layer,
    gain_attn,
    gain_ffn,
    w_query,
    w_key,
    w_value,
    w_out,
    w_gate,
    w_up,
    w_down,
):
    core, x_at, y_at = (lax.axis_index("tp"), lax.axis_index("x"), lax.axis_index("yh"))
    first = core == 0
    rows = tokens.shape[1] // 2
    width = tokens.shape[2]
    keep = keep_layer[0].astype(F32)
    scale = HD ** (-0.5)
    side = x_at // 2
    at = x_at % 2
    wq = half(lax.dynamic_slice_in_dim(w_query, at * 512, 512, axis=1))
    wk = half(lax.dynamic_slice_in_dim(w_key, at * HD, HD, axis=1))
    wv = half(lax.dynamic_slice_in_dim(w_value, at * HD, HD, axis=1))
    wo = half(lax.dynamic_slice_in_dim(w_out, at * 512, 512, axis=1))
    pack0 = jnp.concatenate([wq[:, :256], wk, wo[:, :256]], axis=1)
    pack1 = jnp.concatenate([wq[:, 256:], wv, wo[:, 256:]], axis=1)
    lent = lax.ppermute(
        jnp.where(first, pack1, pack0),
        ("x", "tp"),
        [(2 * i + i // 2, 2 * i + 1 - i // 2) for i in range(4)],
    )
    pack = jnp.where(core == side, jnp.where(first, pack0, pack1), lent)
    pack = lax.all_gather(pack, SHARD, axis=0, tiled=True)
    pack_other = swap_cores(pack)
    att0 = jnp.where(first, pack, pack_other)
    att1 = jnp.where(first, pack_other, pack)
    full_qkv = jnp.concatenate([att0[:, :384], att1[:, :384]], axis=1)
    full_out = jnp.concatenate([att0[:, 384:], att1[:, 384:]], axis=1)
    units = w_gate.shape[1] // 4

    def hidden_units(weight):
        own = half(lax.dynamic_slice_in_dim(weight, x_at * units, units, axis=1))
        own = lax.all_gather(own, SHARD, axis=0, tiled=True)
        return (own, swap_cores(own))

    xval = lax.dynamic_slice_in_dim(tokens[0], core * rows, rows, axis=0).astype(F32)
    grad_top = lax.dynamic_slice_in_dim(cotangent[0], core * rows, rows, axis=0).astype(F32)
    root_attn = norm_root(xval)
    normed_attn = jnp.concatenate(gather_x(half(xval * root_attn * gain_attn)), axis=0)
    count = normed_attn.shape[0]

    def of_positions(line, y_index, core_index):
        grid = line.reshape(2, 4, 2, rows)
        picked = lax.dynamic_index_in_dim(grid, y_index, 0, keepdims=False)
        picked = lax.dynamic_index_in_dim(picked, core_index, 1, keepdims=False)
        double = jnp.concatenate([picked, picked], axis=0)
        return lax.dynamic_slice_in_dim(double, x_at, 4, axis=0).reshape(-1)

    corners = ((y_at, core), (y_at, 1 - core), (1 - y_at, core), (1 - y_at, 1 - core))
    seg_query = of_positions(seq_ids[0], y_at, core)
    blk_query = of_positions(block_ids[0], y_at, core)
    seg_keys = jnp.concatenate([of_positions(seq_ids[0], *corner) for corner in corners])
    blk_keys = jnp.concatenate([of_positions(block_ids[0], *corner) for corner in corners])
    allowed = (seg_query[:, None] == seg_keys[None, :]) & (blk_keys[None, :] <= blk_query[:, None])
    position = of_positions(jnp.arange(seq_ids.shape[1], dtype=jnp.int32), y_at, core)
    freqs = 10000.0 ** (-(jnp.arange(HD // 2).astype(F32) * 2.0 / HD))
    angle = position.astype(F32)[:, None] * freqs[None, :]
    cosine = jnp.concatenate([jnp.cos(angle), jnp.cos(angle)], axis=-1)
    sine = jnp.concatenate([jnp.sin(angle), jnp.sin(angle)], axis=-1)
    qkv = mm(normed_attn, full_qkv)
    starts = (0, 128, 384, 512)
    query = jnp.stack([half(rotate(qkv[:, s : s + HD], cosine, sine)) for s in starts])
    keys_values = jnp.concatenate(
        [half(rotate(qkv[:, 256:384], cosine, sine)), half(qkv[:, 640:])], axis=1
    )

    def across_y(value):
        return lax.ppermute(value, "yh", SWAP)

    two_kv = jnp.concatenate([keys_values, across_y(keys_values)], axis=0)
    other_kv = swap_cores(two_kv)
    all_kv = jnp.concatenate(
        [two_kv[:count], other_kv[:count], two_kv[count:], other_kv[count:]], axis=0
    )
    all_keys, all_values = (all_kv[:, :HD], all_kv[:, HD:])
    raw = jnp.einsum("htd,nd->htn", query, all_keys, preferred_element_type=F32) * scale
    safe = jnp.where(allowed[None], raw, NEG)
    top = jnp.max(safe, axis=-1, keepdims=True)
    weights = jnp.where(allowed[None], jnp.exp(safe - top), 0.0)
    total = jnp.sum(weights, axis=-1, keepdims=True)
    added = jnp.einsum("htn,nd->htd", half(weights), all_values, preferred_element_type=F32)
    heads_f = added / total
    log_total = top + jnp.log(total)
    heads = half(heads_f.transpose(1, 0, 2).reshape(count, 4 * HD))

    def chunked(value):
        return [value[j * rows : (j + 1) * rows] for j in range(4)]

    attn_branch = scatter_x(chunked(mm_nt(heads, full_out)))
    middle = xval + keep * attn_branch
    root_ffn = norm_root(middle)
    normed_ffn = jnp.concatenate(gather_x(half(middle * root_ffn * gain_ffn)), axis=0)
    full_gate, full_up, full_down = (hidden_units(w_gate), hidden_units(w_up), hidden_units(w_down))
    d_ffn = jnp.concatenate(gather_x(half(keep * grad_top)), axis=0)
    branch = 0.0
    d_normed = 0.0
    grads_gate, grads_up, grads_down = ([], [], [])
    for wg, wu, wd in zip(full_gate, full_up, full_down, strict=True):
        gate = mm(normed_ffn, wg)
        up = mm(normed_ffn, wu)
        sig = jax.nn.sigmoid(gate)
        silu = gate * sig
        hidden = half(silu * up)
        branch = branch + mm_nt(hidden, wd)
        d_hidden = mm(d_ffn, wd)
        d_gate = half(d_hidden * up * sig * (1.0 + gate * (1.0 - sig)))
        d_up = half(d_hidden * silu)
        d_normed = d_normed + mm_nt(d_gate, wg) + mm_nt(d_up, wu)
        grads_gate.append(mm_tn(normed_ffn, d_gate))
        grads_up.append(mm_tn(normed_ffn, d_up))
        grads_down.append(mm_tn(d_ffn, hidden))
    d_normed_ffn = scatter_x(chunked(d_normed))
    ffn_branch = scatter_x(chunked(branch))

    def both_cores(value):
        other = swap_cores(value)
        return jnp.concatenate(
            [jnp.where(first, value, other), jnp.where(first, other, value)], axis=0
        )

    output = both_cores(half(middle + keep * ffn_branch))

    def reduce_columns(mine, theirs):
        value = half(mine + swap_cores(half(theirs)).astype(F32))
        value = lax.psum_scatter(value, SHARD, scatter_dimension=0, tiled=True)
        value = half(value.astype(F32) + across_y(value).astype(F32))
        return absolute(gather_x(value), x_at)

    def units_of(value):
        return jnp.concatenate([value[i] for i in range(4)], axis=1).astype(F32)

    grad_down = units_of(reduce_columns(*grads_down))
    grad_gate = units_of(reduce_columns(*grads_gate))
    grad_up = units_of(reduce_columns(*grads_up))
    mid_part, gain_ffn_local = norm_backward(middle, root_ffn, gain_ffn, d_normed_ffn)
    d_middle = grad_top + mid_part
    d_attn = jnp.concatenate(gather_x(half(keep * d_middle)), axis=0)
    d_heads = half(mm(d_attn, full_out))
    d_heads_g = d_heads.reshape(count, 4, HD).transpose(1, 0, 2)
    row_delta = jnp.sum(d_heads_g.astype(F32) * heads_f, axis=-1, keepdims=True)
    raw = jnp.einsum("htd,nd->htn", query, all_keys, preferred_element_type=F32) * scale
    probs = jnp.where(allowed[None], jnp.exp(raw - log_total), 0.0)
    d_probs = jnp.einsum("htd,nd->htn", d_heads_g, all_values, preferred_element_type=F32)
    d_scores = half(scale * probs * (d_probs - row_delta))
    grad_q = jnp.einsum("htn,nd->htd", d_scores, all_keys, preferred_element_type=F32)
    key_part = jnp.einsum("htn,htd->nd", d_scores, query, preferred_element_type=F32)
    value_part = jnp.einsum("htn,htd->nd", half(probs), d_heads_g, preferred_element_type=F32)
    kv_part = jnp.concatenate([key_part, value_part], axis=1)
    kv_mine = jnp.concatenate([kv_part[:count], kv_part[2 * count : 3 * count]], axis=0)
    kv_theirs = jnp.concatenate([kv_part[count : 2 * count], kv_part[3 * count :]], axis=0)
    kv_two = kv_mine + swap_cores(half(kv_theirs)).astype(F32)
    grad_kv = kv_two[:count] + across_y(half(kv_two[count:])).astype(F32)
    d_q = [half(unrotate(grad_q[h], cosine, sine)) for h in range(4)]
    d_key = half(unrotate(grad_kv[:, :HD], cosine, sine))
    d_qkv = jnp.concatenate([d_q[0], d_q[1], d_key, d_q[2], d_q[3], half(grad_kv[:, HD:])], axis=1)
    d_normed_attn = scatter_x(chunked(mm_nt(d_qkv, full_qkv)))
    grad_qkv = mm_tn(normed_attn, d_qkv)
    grad_o = mm_tn(d_attn, heads)
    grads0 = jnp.concatenate([grad_qkv[:, :384], grad_o[:, :256]], axis=1)
    grads1 = jnp.concatenate([grad_qkv[:, 384:], grad_o[:, 256:]], axis=1)
    packs = reduce_columns(jnp.where(first, grads0, grads1), jnp.where(first, grads1, grads0))
    mine = lax.dynamic_slice_in_dim(packs, 2 * core, 2, axis=0)
    theirs = swap_cores(lax.dynamic_slice_in_dim(packs, 2 - 2 * core, 2, axis=0))
    out0 = jnp.where(first, mine, theirs).astype(F32)
    out1 = jnp.where(first, theirs, mine).astype(F32)
    grad_query = jnp.concatenate(
        [out0[0, :, :256], out1[0, :, :256], out0[1, :, :256], out1[1, :, :256]], axis=1
    )
    grad_key = jnp.concatenate([out0[0, :, 256:384], out0[1, :, 256:384]], axis=1)
    grad_value = jnp.concatenate([out1[0, :, 256:384], out1[1, :, 256:384]], axis=1)
    grad_out = jnp.concatenate(
        [out0[0, :, 384:], out1[0, :, 384:], out0[1, :, 384:], out1[1, :, 384:]], axis=1
    )
    input_part, gain_attn_local = norm_backward(xval, root_attn, gain_attn, d_normed_attn)
    input_grad = both_cores(half(d_middle + input_part))
    gains = lax.psum(jnp.stack([gain_attn_local, gain_ffn_local]), ("yl", "z", "yh", "x", "tp"))
    owned = width // 8
    gains = lax.dynamic_slice_in_dim(
        gains, (lax.axis_index("yl") * 4 + lax.axis_index("z")) * owned, owned, axis=1
    )
    return (
        output[None],
        input_grad[None],
        gains[0],
        gains[1],
        grad_query,
        grad_key,
        grad_value,
        grad_out,
        grad_gate,
        grad_up,
        grad_down,
    )


def solution(mesh):
    fine = Mesh(mesh.devices.reshape(2, 4, 2, 4, 2), ("yl", "z", "yh", "x", "tp"))
    shard, ctx = (("yl", "z"), ("yh", "x"))
    acts, weight = (P(shard, ctx, None), P(shard, "tp"))
    return jax.shard_map(
        per_device,
        mesh=fine,
        in_specs=(acts, acts, P(shard, None), P(shard, None), P(shard), P(), P()) + (weight,) * 7,
        out_specs=(acts, acts, P(shard), P(shard)) + (weight,) * 7,
        check_vma=False,
    )
```

profile of v0, /device:TPU:17, one launch (start us, length us, event | category | flops | bytes accessed | tf_op | source)
XLA Modules:
  0.0 724.8 jit_solution(15446372410941713195)
XLA Ops:
  25.9 42.6 %all-gather.5.cloned.1.call-done = bf16[2048,640]{0,1:T(8,128)(2,1)} async-done(((bf16[256,640]{0,1:T(8,128)(2,1)}), bf16[2048,640]{0,1:T(8,128)(2,1)}) %all-gather.5.cloned.1.call-update) | async-done | bytes 2621456 | tf_op jit(solution)/shard_map/all_gather | solution.py:111
  68.4 4.7 collective-permute-start.4
  89.1 12.2 %collective-permute-done.1 = bf16[128,2048]{1,0:T(8,128)(2,1)} collective-permute-done((bf16[128,2048]{1,0:T(8,128)(2,1)}, bf16[128,2048]{1,0:T(8,128)(2,1)}, u32[]{:S(2)}, u32[]{:S(2)}) %collective-permute-start.1) | collective-permute-done | bytes 524320 | tf_op jit(solution)/shard_map/ppermute | solution.py:36
  101.3 3.4 fusion.14
  108.0 12.4 %collective-permute-done.5 = bf16[512,256]{1,0:T(8,128)(2,1)S(1)} collective-permute-done((bf16[512,256]{1,0:T(8,128)(2,1)S(1)}, bf16[512,256]{1,0:T(8,128)(2,1)S(1)}, u32[]{:S(2)}, u32[]{:S(2)}) %collective-permute-start.5) | collective-permute-done | bytes 262176 | tf_op jit(solution)/shard_map/ppermute | solution.py:156
  124.2 2.7 all-gather.11.cloned.1.call-done
  126.9 5.1 collective-permute-start.15
  132.0 48.6 %all-gather.9.cloned.1.call-done = bf16[2048,704]{0,1:T(8,128)(2,1)} async-done(((bf16[256,704]{0,1:T(8,128)(2,1)}), bf16[2048,704]{0,1:T(8,128)(2,1)}) %all-gather.9.cloned.1.call-update) | async-done | bytes 2883600 | tf_op jit(solution)/shard_map/all_gather | solution.py:121
  180.6 4.9 collective-permute-start.14
  192.9 3.6 select_reduce_fusion
  196.5 5.0 fusion.1
  202.3 5.7 fusion.43
  208.0 3.3 fusion.129
  214.9 19.1 %all-gather.7.cloned.1.call-done = bf16[2048,704]{0,1:T(8,128)(2,1)} async-done(((bf16[256,704]{0,1:T(8,128)(2,1)}), bf16[2048,704]{0,1:T(8,128)(2,1)}) %all-gather.7.cloned.1.call-update) | async-done | bytes 2883600 | tf_op jit(solution)/shard_map/all_gather | solution.py:121
  234.0 5.0 collective-permute-start.13
  239.0 2.7 collective-permute-start.7
  243.6 10.8 %collective-permute-done.7 = bf16[128,2048]{1,0:T(8,128)(2,1)} collective-permute-done((bf16[128,2048]{1,0:T(8,128)(2,1)}, bf16[128,2048]{1,0:T(8,128)(2,1)}, u32[]{:S(2)}, u32[]{:S(2)}) %collective-permute-start.7) | collective-permute-done | bytes 524320 | tf_op jit(solution)/shard_map/ppermute | solution.py:36
  254.4 2.7 collective-permute-start.21
  259.2 6.9 collective-permute-done.22
  266.8 10.0 %collective-permute-done.21 = bf16[128,2048]{1,0:T(8,128)(2,1)S(1)} collective-permute-done((bf16[128,2048]{1,0:T(8,128)(2,1)}, bf16[128,2048]{1,0:T(8,128)(2,1)S(1)}, u32[]{:S(2)}, u32[]{:S(2)}) %collective-permute-start.21) | collective-permute-done | bytes 524320 | tf_op jit(solution)/shard_map/ppermute | solution.py:36
  276.8 4.0 collective-permute-done.20
  284.3 3.8 fusion.104
  290.6 11.6 %collective-permute-done.11 = bf16[128,2048]{1,0:T(8,128)(2,1)S(1)} collective-permute-done((bf16[128,2048]{1,0:T(8,128)(2,1)S(1)}, bf16[128,2048]{1,0:T(8,128)(2,1)S(1)}, u32[]{:S(2)}, u32[]{:S(2)}) %collective-permute-start.11) | collective-permute-done | bytes 524320 | tf_op jit(solution)/shard_map/ppermute | solution.py:36
  302.2 4.7 collective-permute-done.10
  307.0 3.7 fusion.106
  310.7 4.2 multiply_convert_fusion.2
  314.9 3.2 convolution_convert_fusion.2
  319.6 3.7 fusion.135
  326.9 3.5 multiply_convert_fusion.3
  334.1 4.1 fusion.112
  338.4 2.8 collective-permute-start.25
  344.4 5.8 fusion.130
  352.8 11.0 %collective-permute-done.25 = bf16[128,2048]{1,0:T(8,128)(2,1)S(1)} collective-permute-done((bf16[128,2048]{1,0:T(8,128)(2,1)S(1)}, bf16[128,2048]{1,0:T(8,128)(2,1)S(1)}, u32[]{:S(2)}, u32[]{:S(2)}) %collective-permute-start.25) | collective-permute-done | bytes 524320 | tf_op jit(solution)/shard_map/ppermute | solution.py:36
  363.8 3.2 collective-permute-done.24
  369.9 4.3 add_convert_fusion.2
  374.3 12.0 %collective-permute-done.18 = bf16[128,2048]{1,0:T(8,128)(2,1)S(1)} collective-permute-done((bf16[128,2048]{1,0:T(8,128)(2,1)}, bf16[128,2048]{1,0:T(8,128)(2,1)S(1)}, u32[]{:S(2)}, u32[]{:S(2)}) %collective-permute-start.18) | collective-permute-done | bytes 524320 | tf_op jit(solution)/shard_map/ppermute | solution.py:36
  386.4 4.6 collective-permute-done.16
  391.0 4.3 multiply_convert_fusion.7
  399.8 2.6 collective-permute-start.46
  402.4 4.5 convolution_convert_fusion
  408.5 14.0 %collective-permute-start.19 = (bf16[128,2048]{1,0:T(8,128)(2,1)}, bf16[128,2048]{1,0:T(8,128)(2,1)}, u32[]{:S(2)}, u32[]{:S(2)}) collective-permute-start(bf16[128,2048]{1,0:T(8,128)(2,1)} %get-tuple-element.127), channel_id=1, source_target_pairs={{0,1},{1,0},{2,3},{3,2},{4,5},{5,4},{6,7},{7,6},{8,9},{9,8},{10,11... | collective-permute-start | bytes 1572872 | tf_op jit(solution)/shard_map/ppermute | solution.py:32
  424.4 12.5 %multiply_convert_fusion = bf16[4,512,2048]{2,1,0:T(8,128)(2,1)} fusion(f32[4,512,2048]{2,1,0:T(8,128)} %copy-done.5, f32[4,512]{1,0:T(4,128)S(1)} %get-tuple-element.171, f32[4,512]{1,0:T(4,128)S(1)} %log_add_fusion, pred[512,2048]{1,0:T(8,128)(4,1)S(1)} %copy-done.13, bf16[4,512,128]{1,2,0:T(8,128)(2,1)S(1)} %bitcast.246, bf16[2048,256]{1,0:T(8,128)(2,1)S(1)} %copy-done.31), kind=kOutput, calls=%fused_computation | convolution fusion | flops 1103101952 | bytes 27279360 | tf_op jit(solution)/shard_map/htd,nd->htn/dot_general | solution.py:231
  436.9 5.8 convolution_bitcast_fusion
  442.8 8.1 %fusion.9 = f32[2048,128]{1,0:T(8,128)S(1)} fusion(bf16[4,512,128]{1,2,0:T(8,128)(2,1)S(1)} %bitcast.247, f32[4,512,2048]{2,1,0:T(8,128)} %copy-done.5, f32[4,512]{1,0:T(4,128)S(1)} %log_add_fusion, pred[512,2048]{1,0:T(8,128)(4,1)S(1)} %copy-done.13), kind=kOutput, calls=%fused_computation.33 | convolution fusion | flops 1090519040 | bytes 19406848 | tf_op jit(solution)/shard_map/htn,htd->nd/dot_general | solution.py:235
  452.9 3.0 add_convert_fusion.1
  465.5 10.9 %collective-permute-done.30 = bf16[512,256]{1,0:T(8,128)(2,1)S(1)} collective-permute-done((bf16[512,256]{1,0:T(8,128)(2,1)S(1)}, bf16[512,256]{1,0:T(8,128)(2,1)S(1)}, u32[]{:S(2)}, u32[]{:S(2)}) %collective-permute-start.30) | collective-permute-done | bytes 262176 | tf_op jit(solution)/shard_map/ppermute | solution.py:156
  479.4 5.5 add_convert_fusion
  486.6 3.2 fusion.131
  489.9 2.7 collective-permute-start.33
  494.1 3.4 fusion.48
  507.5 9.2 %collective-permute-done.31 = bf16[128,2048]{1,0:T(8,128)(2,1)S(1)} collective-permute-done((bf16[128,2048]{1,0:T(8,128)(2,1)S(1)}, bf16[128,2048]{1,0:T(8,128)(2,1)S(1)}, u32[]{:S(2)}, u32[]{:S(2)}) %collective-permute-start.31) | collective-permute-done | bytes 524320 | tf_op jit(solution)/shard_map/ppermute | solution.py:36
  518.7 2.8 collective-permute-start.34
  522.6 70.6 %psum.7 = f32[2,2048]{1,0:T(2,128)S(1)} all-reduce(f32[2,2048]{1,0:T(2,128)S(1)} %pad_maximum_fusion.34), channel_id=1, replica_groups=mesh['yl'=2,'z'=4,'yh'=2,'x'=4,'tp'=2] {'yl','z','yh','x','tp'}, use_global_device_ids=true, to_apply=%region_9.10 | all-reduce | flops 4096 | bytes 32768 | tf_op jit(solution)/shard_map/psum | solution.py:264
  596.6 5.7 add_convert_fusion.3
  602.4 2.6 collective-permute-start.47
  610.1 8.0 %collective-permute-done.47 = bf16[256,704]{0,1:T(8,128)(2,1)S(1)} collective-permute-done((bf16[256,704]{0,1:T(8,128)(2,1)}, bf16[256,704]{0,1:T(8,128)(2,1)S(1)}, u32[]{:S(2)}, u32[]{:S(2)}) %collective-permute-start.47) | collective-permute-done | bytes 360480 | tf_op jit(solution)/shard_map/ppermute | solution.py:156
  618.2 14.8 %collective-permute-done.52 = bf16[256,704]{0,1:T(8,128)(2,1)S(1)} collective-permute-done((bf16[256,704]{0,1:T(8,128)(2,1)}, bf16[256,704]{0,1:T(8,128)(2,1)S(1)}, u32[]{:S(2)}, u32[]{:S(2)}) %collective-permute-start.52) | collective-permute-done | bytes 360480 | tf_op jit(solution)/shard_map/ppermute | solution.py:156
  634.0 2.7 collective-permute-start.53
  640.9 14.2 %collective-permute-done.50 = bf16[256,704]{0,1:T(8,128)(2,1)S(1)} collective-permute-done((bf16[256,704]{0,1:T(8,128)(2,1)S(1)}, bf16[256,704]{0,1:T(8,128)(2,1)S(1)}, u32[]{:S(2)}, u32[]{:S(2)}) %collective-permute-start.50) | collective-permute-done | bytes 360480 | tf_op jit(solution)/shard_map/ppermute | solution.py:36
  659.8 7.6 %collective-permute-done.55 = bf16[256,704]{0,1:T(8,128)(2,1)} collective-permute-done((bf16[256,704]{0,1:T(8,128)(2,1)}, bf16[256,704]{0,1:T(8,128)(2,1)}, u32[]{:S(2)}, u32[]{:S(2)}) %collective-permute-start.55) | collective-permute-done | bytes 360480 | tf_op jit(solution)/shard_map/ppermute | solution.py:36
  674.2 3.5 collective-permute-done.37
  677.7 3.1 collective-permute-done.38
  680.9 9.2 %collective-permute-done.39 = bf16[256,640]{0,1:T(8,128)(2,1)S(1)} collective-permute-done((bf16[256,640]{0,1:T(8,128)(2,1)S(1)}, bf16[256,640]{0,1:T(8,128)(2,1)S(1)}, u32[]{:S(2)}, u32[]{:S(2)}) %collective-permute-start.39) | collective-permute-done | bytes 327712 | tf_op jit(solution)/shard_map/ppermute | solution.py:36
  696.0 3.4 copy.68
  (446 shorter events, 168.1 us)
Async XLA Ops:
  7.2 61.2 %all-gather.5.cloned.1.call-start = ((), (), s32[]{:S(2)}) async-start(), calls=%async_computation.4 | async-start | bytes 2949120 | tf_op jit(solution)/shard_map/all_gather | solution.py:111
  15.8 3.9 collective-permute-start.3
  21.5 105.4 %all-gather.11.cloned.1.call-start = ((), (), s32[]{:S(2)}) async-start(), calls=%async_computation.7 | async-start | bytes 3244032 | tf_op jit(solution)/shard_map/all_gather | solution.py:121
  22.7 157.9 %all-gather.9.cloned.1.call-start = ((), (), s32[]{:S(2)}) async-start(), calls=%async_computation.6 | async-start | bytes 3244032 | tf_op jit(solution)/shard_map/all_gather | solution.py:121
  25.1 208.9 %all-gather.7.cloned.1.call-start = ((), (), s32[]{:S(2)}) async-start(), calls=%async_computation.5 | async-start | bytes 3244032 | tf_op jit(solution)/shard_map/all_gather | solution.py:121
  68.4 14.1 %collective-permute-start.4 = (bf16[2048,640]{0,1:T(8,128)(2,1)}, bf16[2048,640]{0,1:T(8,128)(2,1)}, u32[]{:S(2)}, u32[]{:S(2)}) collective-permute-start(bf16[2048,640]{0,1:T(8,128)(2,1)} %all-gather.5.cloned.1.call-done), channel_id=1, source_target_pairs={{0,1},{1,0},{2,3},{3,2},{4,5},{5,4},{6,7},{7,6},{8,9},{9,8},{10,11... | collective-permute-start | bytes 7864328 | tf_op jit(solution)/shard_map/ppermute | solution.py:32
  74.1 15.1 %collective-permute-start.2 = (bf16[128,2048]{1,0:T(8,128)(2,1)}, bf16[128,2048]{1,0:T(8,128)(2,1)}, u32[]{:S(2)}, u32[]{:S(2)}) collective-permute-start(bf16[128,2048]{1,0:T(8,128)(2,1)} %fusion.23), channel_id=1, source_target_pairs={{0,2},{2,4},{4,6},{6,0},{1,3},{3,5},{5,7},{7,1},{8,10},{10,12},{12... | collective-permute-start | bytes 1572872 | tf_op jit(solution)/shard_map/ppermute | solution.py:36
  75.3 26.0 %collective-permute-start.1 = (bf16[128,2048]{1,0:T(8,128)(2,1)}, bf16[128,2048]{1,0:T(8,128)(2,1)}, u32[]{:S(2)}, u32[]{:S(2)}) collective-permute-start(bf16[128,2048]{1,0:T(8,128)(2,1)} %fusion.23), channel_id=1, source_target_pairs={{0,4},{2,6},{4,0},{6,2},{1,5},{3,7},{5,1},{7,3},{8,12},{10,14},{12... | collective-permute-start | bytes 1572872 | tf_op jit(solution)/shard_map/ppermute | solution.py:36
  77.7 23.6 %collective-permute-start = (bf16[128,2048]{1,0:T(8,128)(2,1)}, bf16[128,2048]{1,0:T(8,128)(2,1)}, u32[]{:S(2)}, u32[]{:S(2)}) collective-permute-start(bf16[128,2048]{1,0:T(8,128)(2,1)} %fusion.23), channel_id=1, source_target_pairs={{0,6},{2,0},{4,2},{6,4},{1,7},{3,1},{5,3},{7,5},{8,14},{10,8},{12,... | collective-permute-start | bytes 1572872 | tf_op jit(solution)/shard_map/ppermute | solution.py:36
  81.1 515.0 %reduce-scatter.7.cloned.1.call-start = ((), (), s32[]{:S(2)}) async-start(), calls=%async_computation.9 | async-start | bytes 3244032 | tf_op jit(solution)/shard_map/reduce_scatter | solution.py:213
  106.7 13.7 %collective-permute-start.5 = (bf16[512,256]{1,0:T(8,128)(2,1)S(1)}, bf16[512,256]{1,0:T(8,128)(2,1)S(1)}, u32[]{:S(2)}, u32[]{:S(2)}) collective-permute-start(bf16[512,256]{1,0:T(8,128)(2,1)S(1)} %pad_maximum_fusion.29), channel_id=1, source_target_pairs={{0,8},{8,0},{1,9},{9,1},{2,10},{10,2},{3,11},{11,3},{4,12},{12,4},... | collective-permute-start | bytes 786440 | tf_op jit(solution)/shard_map/ppermute | solution.py:156
  121.3 70.3 %collective-permute-start.6 = (bf16[1024,256]{1,0:T(8,128)(2,1)}, bf16[1024,256]{1,0:T(8,128)(2,1)}, u32[]{:S(2)}, u32[]{:S(2)}) collective-permute-start(bf16[1024,256]{1,0:T(8,128)(2,1)} %pad_maximum_fusion.19), channel_id=1, source_target_pairs={{0,1},{1,0},{2,3},{3,2},{4,5},{5,4},{6,7},{7,6},{8,9},{9,8},{10,11... | collective-permute-start | bytes 1572872 | tf_op jit(solution)/shard_map/ppermute | solution.py:32
  126.9 155.7 %collective-permute-start.15 = (bf16[2048,704]{0,1:T(8,128)(2,1)}, bf16[2048,704]{0,1:T(8,128)(2,1)}, u32[]{:S(2)}, u32[]{:S(2)}) collective-permute-start(bf16[2048,704]{0,1:T(8,128)(2,1)} %all-gather.11.cloned.1.call-done), channel_id=1, source_target_pairs={{0,1},{1,0},{2,3},{3,2},{4,5},{5,4},{6,7},{7,6},{8,9},{9,8},{10,11... | collective-permute-start | bytes 8650760 | tf_op jit(solution)/shard_map/ppermute | solution.py:32
  180.6 107.6 %collective-permute-start.14 = (bf16[2048,704]{0,1:T(8,128)(2,1)}, bf16[2048,704]{0,1:T(8,128)(2,1)}, u32[]{:S(2)}, u32[]{:S(2)}) collective-permute-start(bf16[2048,704]{0,1:T(8,128)(2,1)} %all-gather.9.cloned.1.call-done), channel_id=1, source_target_pairs={{0,1},{1,0},{2,3},{3,2},{4,5},{5,4},{6,7},{7,6},{8,9},{9,8},{10,11... | collective-permute-start | bytes 8650760 | tf_op jit(solution)/shard_map/ppermute | solution.py:32
  212.5 26.5 %collective-permute-start.9 = (bf16[128,2048]{1,0:T(8,128)(2,1)}, bf16[128,2048]{1,0:T(8,128)(2,1)S(1)}, u32[]{:S(2)}, u32[]{:S(2)}) collective-permute-start(bf16[128,2048]{1,0:T(8,128)(2,1)} %get-tuple-element.91), channel_id=1, source_target_pairs={{0,6},{2,0},{4,2},{6,4},{1,7},{3,1},{5,3},{7,5},{8,14},{10,8},{12,... | collective-permute-start | bytes 1572872 | tf_op jit(solution)/shard_map/ppermute | solution.py:36
  214.9 28.3 %collective-permute-start.8 = (bf16[128,2048]{1,0:T(8,128)(2,1)}, bf16[128,2048]{1,0:T(8,128)(2,1)}, u32[]{:S(2)}, u32[]{:S(2)}) collective-permute-start(bf16[128,2048]{1,0:T(8,128)(2,1)} %get-tuple-element.92), channel_id=1, source_target_pairs={{0,2},{2,4},{4,6},{6,0},{1,3},{3,5},{5,7},{7,1},{8,10},{10,12},{12... | collective-permute-start | bytes 1572872 | tf_op jit(solution)/shard_map/ppermute | solution.py:36
  234.0 76.7 %collective-permute-start.13 = (bf16[2048,704]{0,1:T(8,128)(2,1)}, bf16[2048,704]{0,1:T(8,128)(2,1)}, u32[]{:S(2)}, u32[]{:S(2)}) collective-permute-start(bf16[2048,704]{0,1:T(8,128)(2,1)} %all-gather.7.cloned.1.call-done), channel_id=1, source_target_pairs={{0,1},{1,0},{2,3},{3,2},{4,5},{5,4},{6,7},{7,6},{8,9},{9,8},{10,11... | collective-permute-start | bytes 8650760 | tf_op jit(solution)/shard_map/ppermute | solution.py:32
  239.0 15.4 %collective-permute-start.7 = (bf16[128,2048]{1,0:T(8,128)(2,1)}, bf16[128,2048]{1,0:T(8,128)(2,1)}, u32[]{:S(2)}, u32[]{:S(2)}) collective-permute-start(bf16[128,2048]{1,0:T(8,128)(2,1)} %get-tuple-element.90), channel_id=1, source_target_pairs={{0,4},{2,6},{4,0},{6,2},{1,5},{3,7},{5,1},{7,3},{8,12},{10,14},{12... | collective-permute-start | bytes 1572872 | tf_op jit(solution)/shard_map/ppermute | solution.py:36
  243.3 22.9 %collective-permute-start.22 = (bf16[128,2048]{1,0:T(8,128)(2,1)}, bf16[128,2048]{1,0:T(8,128)(2,1)}, u32[]{:S(2)}, u32[]{:S(2)}) collective-permute-start(bf16[128,2048]{1,0:T(8,128)(2,1)} %fusion.20), channel_id=1, source_target_pairs={{0,2},{2,4},{4,6},{6,0},{1,3},{3,5},{5,7},{7,1},{8,10},{10,12},{12... | collective-permute-start | bytes 1572872 | tf_op jit(solution)/shard_map/ppermute | solution.py:36
  254.4 22.4 %collective-permute-start.21 = (bf16[128,2048]{1,0:T(8,128)(2,1)}, bf16[128,2048]{1,0:T(8,128)(2,1)S(1)}, u32[]{:S(2)}, u32[]{:S(2)}) collective-permute-start(bf16[128,2048]{1,0:T(8,128)(2,1)} %fusion.20), channel_id=1, source_target_pairs={{0,4},{2,6},{4,0},{6,2},{1,5},{3,7},{5,1},{7,3},{8,12},{10,14},{12... | collective-permute-start | bytes 1572872 | tf_op jit(solution)/shard_map/ppermute | solution.py:36
  266.2 14.6 %collective-permute-start.20 = (bf16[128,2048]{1,0:T(8,128)(2,1)}, bf16[128,2048]{1,0:T(8,128)(2,1)S(1)}, u32[]{:S(2)}, u32[]{:S(2)}) collective-permute-start(bf16[128,2048]{1,0:T(8,128)(2,1)} %fusion.20), channel_id=1, source_target_pairs={{0,6},{2,0},{4,2},{6,4},{1,7},{3,1},{5,3},{7,5},{8,14},{10,8},{12,... | collective-permute-start | bytes 1572872 | tf_op jit(solution)/shard_map/ppermute | solution.py:36
  276.8 13.9 %collective-permute-start.12 = (bf16[128,2048]{1,0:T(8,128)(2,1)S(1)}, bf16[128,2048]{1,0:T(8,128)(2,1)S(1)}, u32[]{:S(2)}, u32[]{:S(2)}) collective-permute-start(bf16[128,2048]{1,0:T(8,128)(2,1)S(1)} %multiply_convert_fusion.8), channel_id=1, source_target_pairs={{0,2},{2,4},{4,6},{6,0},{1,3},{3,5},{5,7},{7,1},{8,10},{10,12},{12... | collective-permute-start | bytes 1572872 | tf_op jit(solution)/shard_map/ppermute | solution.py:36
  280.8 21.4 %collective-permute-start.11 = (bf16[128,2048]{1,0:T(8,128)(2,1)S(1)}, bf16[128,2048]{1,0:T(8,128)(2,1)S(1)}, u32[]{:S(2)}, u32[]{:S(2)}) collective-permute-start(bf16[128,2048]{1,0:T(8,128)(2,1)S(1)} %multiply_convert_fusion.8), channel_id=1, source_target_pairs={{0,4},{2,6},{4,0},{6,2},{1,5},{3,7},{5,1},{7,3},{8,12},{10,14},{12... | collective-permute-start | bytes 1572872 | tf_op jit(solution)/shard_map/ppermute | solution.py:36
  282.6 24.4 %collective-permute-start.10 = (bf16[128,2048]{1,0:T(8,128)(2,1)S(1)}, bf16[128,2048]{1,0:T(8,128)(2,1)S(1)}, u32[]{:S(2)}, u32[]{:S(2)}) collective-permute-start(bf16[128,2048]{1,0:T(8,128)(2,1)S(1)} %multiply_convert_fusion.8), channel_id=1, source_target_pairs={{0,6},{2,0},{4,2},{6,4},{1,7},{3,1},{5,3},{7,5},{8,14},{10,8},{12,... | collective-permute-start | bytes 1572872 | tf_op jit(solution)/shard_map/ppermute | solution.py:36
  318.1 51.7 %collective-permute-start.41 = (bf16[2048,704]{0,1:T(8,128)(2,1)}, bf16[2048,704]{0,1:T(8,128)(2,1)}, u32[]{:S(2)}, u32[]{:S(2)}) collective-permute-start(bf16[2048,704]{0,1:T(8,128)(2,1)} %convolution_convert_fusion.2), channel_id=1, source_target_pairs={{0,1},{1,0},{2,3},{3,2},{4,5},{5,4},{6,7},{7,6},{8,9},{9,8},{10,11... | collective-permute-start | bytes 8650760 | tf_op jit(solution)/shard_map/ppermute | solution.py:32
  338.4 25.3 %collective-permute-start.25 = (bf16[128,2048]{1,0:T(8,128)(2,1)S(1)}, bf16[128,2048]{1,0:T(8,128)(2,1)S(1)}, u32[]{:S(2)}, u32[]{:S(2)}) collective-permute-start(bf16[128,2048]{1,0:T(8,128)(2,1)S(1)} %get-tuple-element.85), channel_id=1, source_target_pairs={{0,6},{2,0},{4,2},{6,4},{1,7},{3,1},{5,3},{7,5},{8,14},{10,8},{12,... | collective-permute-start | bytes 1572872 | tf_op jit(solution)/shard_map/ppermute | solution.py:36
  341.3 25.7 %collective-permute-start.24 = (bf16[128,2048]{1,0:T(8,128)(2,1)S(1)}, bf16[128,2048]{1,0:T(8,128)(2,1)S(1)}, u32[]{:S(2)}, u32[]{:S(2)}) collective-permute-start(bf16[128,2048]{1,0:T(8,128)(2,1)S(1)} %get-tuple-element.86), channel_id=1, source_target_pairs={{0,2},{2,4},{4,6},{6,0},{1,3},{3,5},{5,7},{7,1},{8,10},{10,12},{12... | collective-permute-start | bytes 1572872 | tf_op jit(solution)/shard_map/ppermute | solution.py:36
  341.3 27.2 %collective-permute-start.23 = (bf16[128,2048]{1,0:T(8,128)(2,1)S(1)}, bf16[128,2048]{1,0:T(8,128)(2,1)S(1)}, u32[]{:S(2)}, u32[]{:S(2)}) collective-permute-start(bf16[128,2048]{1,0:T(8,128)(2,1)S(1)} %get-tuple-element.84), channel_id=1, source_target_pairs={{0,4},{2,6},{4,0},{6,2},{1,5},{3,7},{5,1},{7,3},{8,12},{10,14},{12... | collective-permute-start | bytes 1572872 | tf_op jit(solution)/shard_map/ppermute | solution.py:36
  351.4 35.0 %collective-permute-start.18 = (bf16[128,2048]{1,0:T(8,128)(2,1)}, bf16[128,2048]{1,0:T(8,128)(2,1)S(1)}, u32[]{:S(2)}, u32[]{:S(2)}) collective-permute-start(bf16[128,2048]{1,0:T(8,128)(2,1)} %get-tuple-element.88), channel_id=1, source_target_pairs={{0,6},{2,0},{4,2},{6,4},{1,7},{3,1},{5,3},{7,5},{8,14},{10,8},{12,... | collective-permute-start | bytes 1572872 | tf_op jit(solution)/shard_map/ppermute | solution.py:36
  363.8 22.6 %collective-permute-start.17 = (bf16[128,2048]{1,0:T(8,128)(2,1)}, bf16[128,2048]{1,0:T(8,128)(2,1)}, u32[]{:S(2)}, u32[]{:S(2)}) collective-permute-start(bf16[128,2048]{1,0:T(8,128)(2,1)} %get-tuple-element.89), channel_id=1, source_target_pairs={{0,2},{2,4},{4,6},{6,0},{1,3},{3,5},{5,7},{7,1},{8,10},{10,12},{12... | collective-permute-start | bytes 1572872 | tf_op jit(solution)/shard_map/ppermute | solution.py:36
  367.0 23.9 %collective-permute-start.16 = (bf16[128,2048]{1,0:T(8,128)(2,1)}, bf16[128,2048]{1,0:T(8,128)(2,1)}, u32[]{:S(2)}, u32[]{:S(2)}) collective-permute-start(bf16[128,2048]{1,0:T(8,128)(2,1)} %get-tuple-element.87), channel_id=1, source_target_pairs={{0,4},{2,6},{4,0},{6,2},{1,5},{3,7},{5,1},{7,3},{8,12},{10,14},{12... | collective-permute-start | bytes 1572872 | tf_op jit(solution)/shard_map/ppermute | solution.py:36
  374.2 228.1 %reduce-scatter.9.cloned.1.call-start = ((), (), s32[]{:S(2)}) async-start(), calls=%async_computation.10 | async-start | bytes 3244032 | tf_op jit(solution)/shard_map/reduce_scatter | solution.py:213
  395.3 13.3 %collective-permute-start.28 = (bf16[128,2048]{1,0:T(8,128)(2,1)S(1)}, bf16[128,2048]{1,0:T(8,128)(2,1)S(1)}, u32[]{:S(2)}, u32[]{:S(2)}) collective-permute-start(bf16[128,2048]{1,0:T(8,128)(2,1)S(1)} %get-tuple-element.46), channel_id=1, source_target_pairs={{0,2},{2,4},{4,6},{6,0},{1,3},{3,5},{5,7},{7,1},{8,10},{10,12},{12... | collective-permute-start | bytes 1572872 | tf_op jit(solution)/shard_map/ppermute | solution.py:36
  395.3 27.2 %collective-permute-start.27 = (bf16[128,2048]{1,0:T(8,128)(2,1)S(1)}, bf16[128,2048]{1,0:T(8,128)(2,1)S(1)}, u32[]{:S(2)}, u32[]{:S(2)}) collective-permute-start(bf16[128,2048]{1,0:T(8,128)(2,1)S(1)} %get-tuple-element.46), channel_id=1, source_target_pairs={{0,4},{2,6},{4,0},{6,2},{1,5},{3,7},{5,1},{7,3},{8,12},{10,14},{12... | collective-permute-start | bytes 1572872 | tf_op jit(solution)/shard_map/ppermute | solution.py:36
  396.1 26.4 %collective-permute-start.26 = (bf16[128,2048]{1,0:T(8,128)(2,1)S(1)}, bf16[128,2048]{1,0:T(8,128)(2,1)S(1)}, u32[]{:S(2)}, u32[]{:S(2)}) collective-permute-start(bf16[128,2048]{1,0:T(8,128)(2,1)S(1)} %get-tuple-element.46), channel_id=1, source_target_pairs={{0,6},{2,0},{4,2},{6,4},{1,7},{3,1},{5,3},{7,5},{8,14},{10,8},{12,... | collective-permute-start | bytes 1572872 | tf_op jit(solution)/shard_map/ppermute | solution.py:36
  399.8 52.3 %collective-permute-start.46 = (bf16[2048,704]{0,1:T(8,128)(2,1)S(1)}, bf16[2048,704]{0,1:T(8,128)(2,1)S(1)}, u32[]{:S(2)}, u32[]{:S(2)}) collective-permute-start(bf16[2048,704]{0,1:T(8,128)(2,1)S(1)} %convolution_convert_fusion.1), channel_id=1, source_target_pairs={{0,1},{1,0},{2,3},{3,2},{4,5},{5,4},{6,7},{7,6},{8,9},{9,8},{10,11... | collective-permute-start | bytes 8650760 | tf_op jit(solution)/shard_map/ppermute | solution.py:32
  406.9 72.5 %collective-permute-start.51 = (bf16[2048,704]{0,1:T(8,128)(2,1)}, bf16[2048,704]{0,1:T(8,128)(2,1)}, u32[]{:S(2)}, u32[]{:S(2)}) collective-permute-start(bf16[2048,704]{0,1:T(8,128)(2,1)} %convolution_convert_fusion), channel_id=1, source_target_pairs={{0,1},{1,0},{2,3},{3,2},{4,5},{5,4},{6,7},{7,6},{8,9},{9,8},{10,11... | collective-permute-start | bytes 8650760 | tf_op jit(solution)/shard_map/ppermute | solution.py:32
  408.5 95.5 %collective-permute-start.19 = (bf16[128,2048]{1,0:T(8,128)(2,1)}, bf16[128,2048]{1,0:T(8,128)(2,1)}, u32[]{:S(2)}, u32[]{:S(2)}) collective-permute-start(bf16[128,2048]{1,0:T(8,128)(2,1)} %get-tuple-element.127), channel_id=1, source_target_pairs={{0,1},{1,0},{2,3},{3,2},{4,5},{5,4},{6,7},{7,6},{8,9},{9,8},{10,11... | collective-permute-start | bytes 1572872 | tf_op jit(solution)/shard_map/ppermute | solution.py:32
  455.9 150.1 %reduce-scatter.11.cloned.1.call-start = ((), (), s32[]{:S(2)}) async-start(), calls=%async_computation.11 | async-start | bytes 3244032 | tf_op jit(solution)/shard_map/reduce_scatter | solution.py:213
  457.2 4.2 collective-permute-start.29
  461.6 14.7 %collective-permute-start.30 = (bf16[512,256]{1,0:T(8,128)(2,1)S(1)}, bf16[512,256]{1,0:T(8,128)(2,1)S(1)}, u32[]{:S(2)}, u32[]{:S(2)}) collective-permute-start(bf16[512,256]{1,0:T(8,128)(2,1)S(1)} %slice.636), channel_id=1, source_target_pairs={{0,8},{8,0},{1,9},{9,1},{2,10},{10,2},{3,11},{11,3},{4,12},{12,4},... | collective-permute-start | bytes 786440 | tf_op jit(solution)/shard_map/ppermute | solution.py:156
  484.9 174.0 %reduce-scatter.5.cloned.1.call-start = ((), (), s32[]{:S(2)}) async-start(), calls=%async_computation.8 | async-start | bytes 2949120 | tf_op jit(solution)/shard_map/reduce_scatter | solution.py:213
  489.9 15.3 %collective-permute-start.33 = (bf16[128,2048]{1,0:T(8,128)(2,1)S(1)}, bf16[128,2048]{1,0:T(8,128)(2,1)S(1)}, u32[]{:S(2)}, u32[]{:S(2)}) collective-permute-start(bf16[128,2048]{1,0:T(8,128)(2,1)S(1)} %get-tuple-element.80), channel_id=1, source_target_pairs={{0,6},{2,0},{4,2},{6,4},{1,7},{3,1},{5,3},{7,5},{8,14},{10,8},{12,... | collective-permute-start | bytes 1572872 | tf_op jit(solution)/shard_map/ppermute | solution.py:36
  492.6 14.8 %collective-permute-start.32 = (bf16[128,2048]{1,0:T(8,128)(2,1)S(1)}, bf16[128,2048]{1,0:T(8,128)(2,1)S(1)}, u32[]{:S(2)}, u32[]{:S(2)}) collective-permute-start(bf16[128,2048]{1,0:T(8,128)(2,1)S(1)} %get-tuple-element.81), channel_id=1, source_target_pairs={{0,2},{2,4},{4,6},{6,0},{1,3},{3,5},{5,7},{7,1},{8,10},{10,12},{12... | collective-permute-start | bytes 1572872 | tf_op jit(solution)/shard_map/ppermute | solution.py:36
  492.7 24.0 %collective-permute-start.31 = (bf16[128,2048]{1,0:T(8,128)(2,1)S(1)}, bf16[128,2048]{1,0:T(8,128)(2,1)S(1)}, u32[]{:S(2)}, u32[]{:S(2)}) collective-permute-start(bf16[128,2048]{1,0:T(8,128)(2,1)S(1)} %get-tuple-element.79), channel_id=1, source_target_pairs={{0,4},{2,6},{4,0},{6,2},{1,5},{3,7},{5,1},{7,3},{8,12},{10,14},{12... | collective-permute-start | bytes 1572872 | tf_op jit(solution)/shard_map/ppermute | solution.py:36
  502.9 93.7 %collective-permute-start.35 = (bf16[2048,640]{0,1:T(8,128)(2,1)}, bf16[2048,640]{0,1:T(8,128)(2,1)}, u32[]{:S(2)}, u32[]{:S(2)}) collective-permute-start(bf16[2048,640]{0,1:T(8,128)(2,1)} %select_convert_fusion), channel_id=1, source_target_pairs={{0,1},{1,0},{2,3},{3,2},{4,5},{5,4},{6,7},{7,6},{8,9},{9,8},{10,11... | collective-permute-start | bytes 7864328 | tf_op jit(solution)/shard_map/ppermute | solution.py:32
  518.7 75.1 %collective-permute-start.34 = (bf16[128,2048]{1,0:T(8,128)(2,1)}, bf16[128,2048]{1,0:T(8,128)(2,1)}, u32[]{:S(2)}, u32[]{:S(2)}) collective-permute-start(bf16[128,2048]{1,0:T(8,128)(2,1)} %fusion.27), channel_id=1, source_target_pairs={{0,1},{1,0},{2,3},{3,2},{4,5},{5,4},{6,7},{7,6},{8,9},{9,8},{10,11... | collective-permute-start | bytes 1572872 | tf_op jit(solution)/shard_map/ppermute | solution.py:32
  596.1 11.0 %collective-permute-start.42 = (bf16[256,704]{0,1:T(8,128)(2,1)}, bf16[256,704]{0,1:T(8,128)(2,1)S(1)}, u32[]{:S(2)}, u32[]{:S(2)}) collective-permute-start(bf16[256,704]{0,1:T(8,128)(2,1)} %reduce-scatter.7.cloned.1.call-done), channel_id=1, source_target_pairs={{0,8},{8,0},{1,9},{9,1},{2,10},{10,2},{3,11},{11,3},{4,12},{12,4},... | collective-permute-start | bytes 1081352 | tf_op jit(solution)/shard_map/ppermute | solution.py:156
  602.4 15.6 %collective-permute-start.47 = (bf16[256,704]{0,1:T(8,128)(2,1)}, bf16[256,704]{0,1:T(8,128)(2,1)S(1)}, u32[]{:S(2)}, u32[]{:S(2)}) collective-permute-start(bf16[256,704]{0,1:T(8,128)(2,1)} %reduce-scatter.9.cloned.1.call-done), channel_id=1, source_target_pairs={{0,8},{8,0},{1,9},{9,1},{2,10},{10,2},{3,11},{11,3},{4,12},{12,4},... | collective-permute-start | bytes 1081352 | tf_op jit(solution)/shard_map/ppermute | solution.py:156
  606.0 27.0 %collective-permute-start.52 = (bf16[256,704]{0,1:T(8,128)(2,1)}, bf16[256,704]{0,1:T(8,128)(2,1)S(1)}, u32[]{:S(2)}, u32[]{:S(2)}) collective-permute-start(bf16[256,704]{0,1:T(8,128)(2,1)} %reduce-scatter.11.cloned.1.call-done), channel_id=1, source_target_pairs={{0,8},{8,0},{1,9},{9,1},{2,10},{10,2},{3,11},{11,3},{4,12},{12,4},... | collective-permute-start | bytes 1081352 | tf_op jit(solution)/shard_map/ppermute | solution.py:156
  607.2 26.8 %collective-permute-start.43 = (bf16[256,704]{0,1:T(8,128)(2,1)S(1)}, bf16[256,704]{0,1:T(8,128)(2,1)S(1)}, u32[]{:S(2)}, u32[]{:S(2)}) collective-permute-start(bf16[256,704]{0,1:T(8,128)(2,1)S(1)} %get-tuple-element.42), channel_id=1, source_target_pairs={{0,6},{2,0},{4,2},{6,4},{1,7},{3,1},{5,3},{7,5},{8,14},{10,8},{12,... | collective-permute-start | bytes 1081352 | tf_op jit(solution)/shard_map/ppermute | solution.py:36
  608.0 26.1 %collective-permute-start.44 = (bf16[256,704]{0,1:T(8,128)(2,1)S(1)}, bf16[256,704]{0,1:T(8,128)(2,1)S(1)}, u32[]{:S(2)}, u32[]{:S(2)}) collective-permute-start(bf16[256,704]{0,1:T(8,128)(2,1)S(1)} %get-tuple-element.42), channel_id=1, source_target_pairs={{0,4},{2,6},{4,0},{6,2},{1,5},{3,7},{5,1},{7,3},{8,12},{10,14},{12... | collective-permute-start | bytes 1081352 | tf_op jit(solution)/shard_map/ppermute | solution.py:36
  609.3 27.5 %collective-permute-start.45 = (bf16[256,704]{0,1:T(8,128)(2,1)S(1)}, bf16[256,704]{0,1:T(8,128)(2,1)S(1)}, u32[]{:S(2)}, u32[]{:S(2)}) collective-permute-start(bf16[256,704]{0,1:T(8,128)(2,1)S(1)} %get-tuple-element.42), channel_id=1, source_target_pairs={{0,2},{2,4},{4,6},{6,0},{1,3},{3,5},{5,7},{7,1},{8,10},{10,12},{12... | collective-permute-start | bytes 1081352 | tf_op jit(solution)/shard_map/ppermute | solution.py:36
  618.1 20.7 %collective-permute-start.48 = (bf16[256,704]{0,1:T(8,128)(2,1)S(1)}, bf16[256,704]{0,1:T(8,128)(2,1)S(1)}, u32[]{:S(2)}, u32[]{:S(2)}) collective-permute-start(bf16[256,704]{0,1:T(8,128)(2,1)S(1)} %get-tuple-element.40), channel_id=1, source_target_pairs={{0,6},{2,0},{4,2},{6,4},{1,7},{3,1},{5,3},{7,5},{8,14},{10,8},{12,... | collective-permute-start | bytes 1081352 | tf_op jit(solution)/shard_map/ppermute | solution.py:36
  633.0 7.9 %collective-permute-start.49 = (bf16[256,704]{0,1:T(8,128)(2,1)S(1)}, bf16[256,704]{0,1:T(8,128)(2,1)S(1)}, u32[]{:S(2)}, u32[]{:S(2)}) collective-permute-start(bf16[256,704]{0,1:T(8,128)(2,1)S(1)} %get-tuple-element.40), channel_id=1, source_target_pairs={{0,4},{2,6},{4,0},{6,2},{1,5},{3,7},{5,1},{7,3},{8,12},{10,14},{12... | collective-permute-start | bytes 1081352 | tf_op jit(solution)/shard_map/ppermute | solution.py:36
  634.0 21.2 %collective-permute-start.50 = (bf16[256,704]{0,1:T(8,128)(2,1)S(1)}, bf16[256,704]{0,1:T(8,128)(2,1)S(1)}, u32[]{:S(2)}, u32[]{:S(2)}) collective-permute-start(bf16[256,704]{0,1:T(8,128)(2,1)S(1)} %get-tuple-element.40), channel_id=1, source_target_pairs={{0,2},{2,4},{4,6},{6,0},{1,3},{3,5},{5,7},{7,1},{8,10},{10,12},{12... | collective-permute-start | bytes 1081352 | tf_op jit(solution)/shard_map/ppermute | solution.py:36
  634.0 23.4 %collective-permute-start.53 = (bf16[256,704]{0,1:T(8,128)(2,1)}, bf16[256,704]{0,1:T(8,128)(2,1)S(1)}, u32[]{:S(2)}, u32[]{:S(2)}) collective-permute-start(bf16[256,704]{0,1:T(8,128)(2,1)} %get-tuple-element.38), channel_id=1, source_target_pairs={{0,6},{2,0},{4,2},{6,4},{1,7},{3,1},{5,3},{7,5},{8,14},{10,8},{12,... | collective-permute-start | bytes 1081352 | tf_op jit(solution)/shard_map/ppermute | solution.py:36
  636.8 22.2 %collective-permute-start.54 = (bf16[256,704]{0,1:T(8,128)(2,1)}, bf16[256,704]{0,1:T(8,128)(2,1)S(1)}, u32[]{:S(2)}, u32[]{:S(2)}) collective-permute-start(bf16[256,704]{0,1:T(8,128)(2,1)} %get-tuple-element.38), channel_id=1, source_target_pairs={{0,4},{2,6},{4,0},{6,2},{1,5},{3,7},{5,1},{7,3},{8,12},{10,14},{12... | collective-permute-start | bytes 1081352 | tf_op jit(solution)/shard_map/ppermute | solution.py:36
  638.8 28.6 %collective-permute-start.55 = (bf16[256,704]{0,1:T(8,128)(2,1)}, bf16[256,704]{0,1:T(8,128)(2,1)}, u32[]{:S(2)}, u32[]{:S(2)}) collective-permute-start(bf16[256,704]{0,1:T(8,128)(2,1)} %get-tuple-element.38), channel_id=1, source_target_pairs={{0,2},{2,4},{4,6},{6,0},{1,3},{3,5},{5,7},{7,1},{8,10},{10,12},{12... | collective-permute-start | bytes 1081352 | tf_op jit(solution)/shard_map/ppermute | solution.py:36
  659.0 10.1 %collective-permute-start.36 = (bf16[256,640]{0,1:T(8,128)(2,1)}, bf16[256,640]{0,1:T(8,128)(2,1)S(1)}, u32[]{:S(2)}, u32[]{:S(2)}) collective-permute-start(bf16[256,640]{0,1:T(8,128)(2,1)} %reduce-scatter.5.cloned.1.call-done), channel_id=1, source_target_pairs={{0,8},{8,0},{1,9},{9,1},{2,10},{10,2},{3,11},{11,3},{4,12},{12,4},... | collective-permute-start | bytes 983048 | tf_op jit(solution)/shard_map/ppermute | solution.py:156
  670.2 7.5 %collective-permute-start.37 = (bf16[256,640]{0,1:T(8,128)(2,1)S(1)}, bf16[256,640]{0,1:T(8,128)(2,1)S(1)}, u32[]{:S(2)}, u32[]{:S(2)}) collective-permute-start(bf16[256,640]{0,1:T(8,128)(2,1)S(1)} %get-tuple-element.44), channel_id=1, source_target_pairs={{0,6},{2,0},{4,2},{6,4},{1,7},{3,1},{5,3},{7,5},{8,14},{10,8},{12,... | collective-permute-start | bytes 983048 | tf_op jit(solution)/shard_map/ppermute | solution.py:36
  672.0 8.9 %collective-permute-start.38 = (bf16[256,640]{0,1:T(8,128)(2,1)S(1)}, bf16[256,640]{0,1:T(8,128)(2,1)S(1)}, u32[]{:S(2)}, u32[]{:S(2)}) collective-permute-start(bf16[256,640]{0,1:T(8,128)(2,1)S(1)} %get-tuple-element.44), channel_id=1, source_target_pairs={{0,4},{2,6},{4,0},{6,2},{1,5},{3,7},{5,1},{7,3},{8,12},{10,14},{12... | collective-permute-start | bytes 983048 | tf_op jit(solution)/shard_map/ppermute | solution.py:36
  672.7 17.3 %collective-permute-start.39 = (bf16[256,640]{0,1:T(8,128)(2,1)S(1)}, bf16[256,640]{0,1:T(8,128)(2,1)S(1)}, u32[]{:S(2)}, u32[]{:S(2)}) collective-permute-start(bf16[256,640]{0,1:T(8,128)(2,1)S(1)} %get-tuple-element.44), channel_id=1, source_target_pairs={{0,2},{2,4},{4,6},{6,0},{1,3},{3,5},{5,7},{7,1},{8,10},{10,12},{12... | collective-permute-start | bytes 983048 | tf_op jit(solution)/shard_map/ppermute | solution.py:36
  692.4 10.8 %collective-permute-start.40 = (bf16[2,256,640]{1,2,0:T(8,128)(2,1)}, bf16[2,256,640]{1,2,0:T(8,128)(2,1)}, u32[]{:S(2)}, u32[]{:S(2)}) collective-permute-start(bf16[2,256,640]{1,2,0:T(8,128)(2,1)} %constant_dynamic-slice_fusion.1), channel_id=1, source_target_pairs={{0,1},{1,0},{2,3},{3,2},{4,5},{5,4},{6,7},{7,6},{8,9},{9,8},{10,11... | collective-permute-start | bytes 1966088 | tf_op jit(solution)/shard_map/ppermute | solution.py:32
  (94 other events, 1312.5 us)
Sparse Core Ops, SparseCore 0:
  21.6 46.7 all-gather.4
  70.6 56.2 all-gather.10
  129.0 51.5 all-gather.8
  182.6 51.3 all-gather.6
  374.4 41.6 reduce-scatter.6
  456.0 44.1 reduce-scatter.8
  503.2 44.1 reduce-scatter.10
  602.5 46.9 reduce-scatter.4
where the time goes:
time: 734 us; the launch traced here: 725 us
  waiting for transfers between devices  310 us (42%)
  matrix products  114 us (16%)
  starting transfers between devices  91.1 us (12%)
  blocking collectives  70.6 us (10%)
  local copies, waits for them, and re-layouts  64.2 us (9%)
  other arithmetic  58.3 us (8%)
  between operations  17 us (2%)
    ppermute x36, waiting for transfers between devices, shift_x(): return lax.ppermute(value, 'x', [(i, (i + hop) % 4) for i in range(4)])  148 us
    psum x1, blocking collectives, per_device(): lax.psum(jnp.stack([gain_attn_local, gain_ffn_local]), ('yl', 'z', 'yh',...  70.6 us
    all_gather x3, waiting for transfers between devices, hidden_units(): own = lax.all_gather(own, SHARD, axis=0, tiled=True)  70.4 us
    ppermute x6, waiting for transfers between devices, across_y(): return lax.ppermute(value, 'yh', SWAP)  46.1 us
    ppermute x13, starting transfers between devices, swap_cores(): return lax.ppermute(value, 'tp', SWAP)  43.7 us
    all_gather x1, waiting for transfers between devices, per_device(): pack = lax.all_gather(pack, SHARD, axis=0, tiled=True)  42.6 us
    ppermute x36, starting transfers between devices, shift_x(): return lax.ppermute(value, 'x', [(i, (i + hop) % 4) for i in range(4)])  40.2 us
    unnamed x222, local copies, waits for them, and re-layouts  38.6 us
  transfers between devices with their start and end apart: 64, of which 31 were waited for; matrix products, arithmetic and copies ran while one was open for 26% of the time, Pallas kernels for 0%

commit v1 on v0

--- a/solution.py
+++ b/solution.py
@@ -261,7 +261,10 @@
     )
     input_part, gain_attn_local = norm_backward(xval, root_attn, gain_attn, d_normed_attn)
     input_grad = both_cores(half(d_middle + input_part))
-    gains = lax.psum(jnp.stack([gain_attn_local, gain_ffn_local]), ("yl", "z", "yh", "x", "tp"))
+    gains = jnp.sum(
+        lax.all_gather(jnp.stack([gain_attn_local, gain_ffn_local]), ("yl", "z", "yh", "x", "tp")),
+        axis=0,
+    )
     owned = width // 8
     gains = lax.dynamic_slice_in_dim(
         gains, (lax.axis_index("yl") * 4 + lax.axis_index("z")) * owned, owned, axis=1

time: 734 us -> 882 us (1.20)
  waiting for transfers between devices: 310 us -> 533 us
  blocking collectives: 70.6 us -> 0 us
    all_gather x0 -> x1, waiting for transfers between devices: none -> 147 us  [per_device(): lax.all_gather(jnp.stack([gain_attn_local, gain_ffn_local]), ('yl', 'z',...]
    reduce_scatter x4, waiting for transfers between devices: 0.03 us -> 90.5 us  [reduce_columns(): value = lax.psum_scatter(value, SHARD, scatter_dimension=0, tiled=True)]
    psum x1 -> x0, blocking collectives: 70.6 us -> none  [per_device(): lax.psum(jnp.stack([gain_attn_local, gain_ffn_local]), ('yl', 'z', 'yh',...]
    ppermute x6, waiting for transfers between devices: 46.1 us -> 18.5 us  [across_y(): return lax.ppermute(value, 'yh', SWAP)]
    ppermute x13, waiting for transfers between devices: 0.03 us -> 11.3 us  [swap_cores(): return lax.ppermute(value, 'tp', SWAP)]
    ppermute x36, waiting for transfers between devices: 148 us -> 157 us  [shift_x(): return lax.ppermute(value, 'x', [(i, (i + hop) % 4) for i in range(4)])]
    unnamed x222 -> x218, local copies, waits for them, and re-layouts: 38.6 us -> 34.7 us
  transfers between devices with their start and end apart: 64 -> 65, of which waited for: 31 -> 40; matrix products, arithmetic and copies ran while one was open for 26% -> 20% of each run, Pallas kernels for 0% -> 0%
where the time goes in v1:
time: 882 us; the launch traced here: 870 us
  waiting for transfers between devices  533 us (60%)
  matrix products  111 us (13%)
  starting transfers between devices  94.4 us (11%)
  other arithmetic  58.8 us (7%)
  local copies, waits for them, and re-layouts  56 us (6%)
  between operations  16.7 us (2%)
    ppermute x36, waiting for transfers between devices, shift_x(): return lax.ppermute(value, 'x', [(i, (i + hop) % 4) for i in range(4)])  157 us
    all_gather x1, waiting for transfers between devices, per_device(): lax.all_gather(jnp.stack([gain_attn_local, gain_ffn_local]), ('yl', 'z',...  147 us
    reduce_scatter x4, waiting for transfers between devices, reduce_columns(): value = lax.psum_scatter(value, SHARD, scatter_dimension=0, tiled=True)  90.5 us
    all_gather x3, waiting for transfers between devices, hidden_units(): own = lax.all_gather(own, SHARD, axis=0, tiled=True)  63.2 us
    ppermute x36, starting transfers between devices, shift_x(): return lax.ppermute(value, 'x', [(i, (i + hop) % 4) for i in range(4)])  47 us
    all_gather x1, waiting for transfers between devices, per_device(): pack = lax.all_gather(pack, SHARD, axis=0, tiled=True)  42.6 us
    ppermute x13, starting transfers between devices, swap_cores(): return lax.ppermute(value, 'tp', SWAP)  41.2 us
    unnamed x218, local copies, waits for them, and re-layouts  34.7 us
  transfers between devices with their start and end apart: 65, of which 40 were waited for; matrix products, arithmetic and copies ran while one was open for 20% of the time, Pallas kernels for 0%

profile of v1, /device:TPU:17, one launch (start us, length us, event | category | flops | bytes accessed | tf_op | source)
XLA Modules:
  0.0 870.0 jit_solution(6439129017536875828)
XLA Ops:
  25.9 42.6 %all-gather.8.cloned.1.call-done = bf16[2048,640]{0,1:T(8,128)(2,1)} async-done(((bf16[256,640]{0,1:T(8,128)(2,1)}), bf16[2048,640]{0,1:T(8,128)(2,1)}) %all-gather.8.cloned.1.call-update) | async-done | bytes 2621456 | tf_op jit(solution)/shard_map/all_gather | solution.py:111
  68.4 4.7 collective-permute-start.4
  85.0 4.2 collective-permute-done.2
  89.2 12.2 %collective-permute-done.1 = bf16[128,2048]{1,0:T(8,128)(2,1)} collective-permute-done((bf16[128,2048]{1,0:T(8,128)(2,1)}, bf16[128,2048]{1,0:T(8,128)(2,1)}, u32[]{:S(2)}, u32[]{:S(2)}) %collective-permute-start.1) | collective-permute-done | bytes 524320 | tf_op jit(solution)/shard_map/ppermute | solution.py:36
  101.4 3.4 fusion.14
  108.1 12.3 %collective-permute-done.5 = bf16[512,256]{1,0:T(8,128)(2,1)S(1)} collective-permute-done((bf16[512,256]{1,0:T(8,128)(2,1)S(1)}, bf16[512,256]{1,0:T(8,128)(2,1)S(1)}, u32[]{:S(2)}, u32[]{:S(2)}) %collective-permute-start.5) | collective-permute-done | bytes 262176 | tf_op jit(solution)/shard_map/ppermute | solution.py:156
  124.2 2.6 all-gather.14.cloned.1.call-done
  126.8 5.7 collective-permute-start.15
  138.6 3.6 select_reduce_fusion
  142.2 5.0 fusion.1
  148.0 5.8 fusion.43
  153.8 3.3 fusion.129
  162.2 17.7 %all-gather.12.cloned.1.call-done = bf16[2048,704]{0,1:T(8,128)(2,1)} async-done(((bf16[256,704]{0,1:T(8,128)(2,1)}), bf16[2048,704]{0,1:T(8,128)(2,1)}) %all-gather.12.cloned.1.call-update) | async-done | bytes 2883600 | tf_op jit(solution)/shard_map/all_gather | solution.py:121
  179.9 5.0 collective-permute-start.14
  190.0 42.8 %all-gather.10.cloned.1.call-done = bf16[2048,704]{0,1:T(8,128)(2,1)} async-done(((bf16[256,704]{0,1:T(8,128)(2,1)}), bf16[2048,704]{0,1:T(8,128)(2,1)}) %all-gather.10.cloned.1.call-update) | async-done | bytes 2883600 | tf_op jit(solution)/shard_map/all_gather | solution.py:121
  232.8 5.1 collective-permute-start.13
  242.7 11.4 %collective-permute-done.20 = bf16[128,2048]{1,0:T(8,128)(2,1)S(1)} collective-permute-done((bf16[128,2048]{1,0:T(8,128)(2,1)}, bf16[128,2048]{1,0:T(8,128)(2,1)S(1)}, u32[]{:S(2)}, u32[]{:S(2)}) %collective-permute-start.20) | collective-permute-done | bytes 524320 | tf_op jit(solution)/shard_map/ppermute | solution.py:36
  257.5 4.0 fusion.104
  261.5 6.7 collective-permute-done.11
  268.3 12.2 %collective-permute-done.10 = bf16[128,2048]{1,0:T(8,128)(2,1)S(1)} collective-permute-done((bf16[128,2048]{1,0:T(8,128)(2,1)S(1)}, bf16[128,2048]{1,0:T(8,128)(2,1)S(1)}, u32[]{:S(2)}, u32[]{:S(2)}) %collective-permute-start.10) | collective-permute-done | bytes 524320 | tf_op jit(solution)/shard_map/ppermute | solution.py:36
  283.9 3.5 fusion.106
  287.5 3.7 multiply_convert_fusion.2
  293.5 3.6 multiply_convert_fusion.3
  300.9 4.1 fusion.112
  305.2 3.2 collective-permute-start.25
  311.7 3.8 fusion.130
  317.8 10.3 %collective-permute-done.25 = bf16[128,2048]{1,0:T(8,128)(2,1)S(1)} collective-permute-done((bf16[128,2048]{1,0:T(8,128)(2,1)S(1)}, bf16[128,2048]{1,0:T(8,128)(2,1)S(1)}, u32[]{:S(2)}, u32[]{:S(2)}) %collective-permute-start.25) | collective-permute-done | bytes 524320 | tf_op jit(solution)/shard_map/ppermute | solution.py:36
  328.1 4.1 collective-permute-done.23
  332.7 19.7 %collective-permute-done.18 = bf16[128,2048]{1,0:T(8,128)(2,1)S(1)} collective-permute-done((bf16[128,2048]{1,0:T(8,128)(2,1)S(1)}, bf16[128,2048]{1,0:T(8,128)(2,1)S(1)}, u32[]{:S(2)}, u32[]{:S(2)}) %collective-permute-start.18) | collective-permute-done | bytes 524320 | tf_op jit(solution)/shard_map/ppermute | solution.py:36
  360.5 3.3 convolution_convert_fusion.2
  363.8 2.8 collective-permute-start.41
  368.3 12.5 %collective-permute-done.27 = bf16[128,2048]{1,0:T(8,128)(2,1)S(1)} collective-permute-done((bf16[128,2048]{1,0:T(8,128)(2,1)S(1)}, bf16[128,2048]{1,0:T(8,128)(2,1)S(1)}, u32[]{:S(2)}, u32[]{:S(2)}) %collective-permute-start.27) | collective-permute-done | bytes 524320 | tf_op jit(solution)/shard_map/ppermute | solution.py:36
  384.2 12.5 %multiply_convert_fusion = bf16[4,512,2048]{2,1,0:T(8,128)(2,1)} fusion(f32[4,512,2048]{2,1,0:T(8,128)} %copy-done.8, f32[4,512]{1,0:T(4,128)S(1)} %get-tuple-element.171, f32[4,512]{1,0:T(4,128)S(1)} %log_add_fusion, pred[512,2048]{1,0:T(8,128)(4,1)S(1)} %copy-done.17, bf16[4,512,128]{1,2,0:T(8,128)(2,1)S(1)} %bitcast.248, bf16[2048,256]{1,0:T(8,128)(2,1)S(1)} %copy-done.41), kind=kOutput, calls=%fused_computation | convolution fusion | flops 1103101952 | bytes 27279360 | tf_op jit(solution)/shard_map/htd,nd->htn/dot_general | solution.py:231
  396.8 5.9 convolution_bitcast_fusion
  402.6 8.1 fusion.9
  414.2 3.0 add_convert_fusion.2
  419.9 6.0 fusion.46
  425.9 4.7 collective-permute-done.30
  438.9 8.7 %collective-permute-done.33 = bf16[128,2048]{1,0:T(8,128)(2,1)S(1)} collective-permute-done((bf16[128,2048]{1,0:T(8,128)(2,1)S(1)}, bf16[128,2048]{1,0:T(8,128)(2,1)S(1)}, u32[]{:S(2)}, u32[]{:S(2)}) %collective-permute-start.33) | collective-permute-done | bytes 524320 | tf_op jit(solution)/shard_map/ppermute | solution.py:36
  447.6 3.9 collective-permute-done.32
  451.5 9.0 %collective-permute-done.31 = bf16[128,2048]{1,0:T(8,128)(2,1)S(1)} collective-permute-done((bf16[128,2048]{1,0:T(8,128)(2,1)S(1)}, bf16[128,2048]{1,0:T(8,128)(2,1)S(1)}, u32[]{:S(2)}, u32[]{:S(2)}) %collective-permute-start.31) | collective-permute-done | bytes 524320 | tf_op jit(solution)/shard_map/ppermute | solution.py:36
  462.7 2.8 convolution_convert_fusion.1
  465.5 4.0 collective-permute-start.46
  469.5 4.9 collective-permute-done.46
  474.4 3.0 add_convert_fusion.1
  478.7 3.0 convolution_convert_fusion
  482.4 4.9 collective-permute-done.51
  487.3 4.7 add_convert_fusion
  496.0 4.9 fusion.48
  501.6 2.6 select_convert_fusion
  511.2 4.1 add_convert_fusion.3
  517.7 147.3 %all-gather.16.cloned.1.call-done = f32[128,2,2048]{2,1,0:T(2,128)} async-done(((f32[1,2,2048]{2,1,0:T(2,128)}), f32[128,2,2048]{2,1,0:T(2,128)}) %all-gather.16.cloned.1.call-update) | async-done | bytes 2097168 | tf_op jit(solution)/shard_map/all_gather | solution.py:265
  667.1 42.0 %reduce-scatter.9.cloned.1.call-done = bf16[256,704]{0,1:T(8,128)(2,1)} async-done(((bf16[2048,704]{0,1:T(8,128)(2,1)}), bf16[256,704]{0,1:T(8,128)(2,1)}) %reduce-scatter.9.cloned.1.call-update) | async-done | bytes 360464 | tf_op jit(solution)/shard_map/reduce_scatter | solution.py:213
  710.2 46.5 %reduce-scatter.11.cloned.1.call-done = bf16[256,704]{0,1:T(8,128)(2,1)} async-done(((bf16[2048,704]{0,1:T(8,128)(2,1)}), bf16[256,704]{0,1:T(8,128)(2,1)}) %reduce-scatter.11.cloned.1.call-update) | async-done | bytes 360464 | tf_op jit(solution)/shard_map/reduce_scatter | solution.py:213
  764.7 2.7 collective-permute-start.49
  768.8 3.9 collective-permute-start.53
  772.7 8.4 collective-permute-done.45
  781.2 2.6 collective-permute-done.48
  784.0 11.5 %collective-permute-done.50 = bf16[256,704]{0,1:T(8,128)(2,1)S(1)} collective-permute-done((bf16[256,704]{0,1:T(8,128)(2,1)S(1)}, bf16[256,704]{0,1:T(8,128)(2,1)S(1)}, u32[]{:S(2)}, u32[]{:S(2)}) %collective-permute-start.50) | collective-permute-done | bytes 360480 | tf_op jit(solution)/shard_map/ppermute | solution.py:36
  804.1 3.8 collective-permute-done.55
  817.6 3.7 collective-permute-done.37
  823.1 3.4 collective-permute-done.39
  828.9 9.7 %collective-permute-start.40 = (bf16[2,256,640]{1,2,0:T(8,128)(2,1)}, bf16[2,256,640]{1,2,0:T(8,128)(2,1)}, u32[]{:S(2)}, u32[]{:S(2)}) collective-permute-start(bf16[2,256,640]{1,2,0:T(8,128)(2,1)} %constant_dynamic-slice_fusion.1), channel_id=1, source_target_pairs={{0,1},{1,0},{2,3},{3,2},{4,5},{5,4},{6,7},{7,6},{8,9},{9,8},{10,11... | collective-permute-start | bytes 1966088 | tf_op jit(solution)/shard_map/ppermute | solution.py:32
  841.5 3.4 copy.68
  (444 shorter events, 179.1 us)
Async XLA Ops:
  7.2 61.2 %all-gather.8.cloned.1.call-start = ((), (), s32[]{:S(2)}) async-start(), calls=%async_computation.4 | async-start | bytes 2949120 | tf_op jit(solution)/shard_map/all_gather | solution.py:111
  15.8 3.9 collective-permute-start.3
  21.5 105.3 %all-gather.14.cloned.1.call-start = ((), (), s32[]{:S(2)}) async-start(), calls=%async_computation.7 | async-start | bytes 3244032 | tf_op jit(solution)/shard_map/all_gather | solution.py:121
  22.7 157.2 %all-gather.12.cloned.1.call-start = ((), (), s32[]{:S(2)}) async-start(), calls=%async_computation.6 | async-start | bytes 3244032 | tf_op jit(solution)/shard_map/all_gather | solution.py:121
  25.1 207.8 %all-gather.10.cloned.1.call-start = ((), (), s32[]{:S(2)}) async-start(), calls=%async_computation.5 | async-start | bytes 3244032 | tf_op jit(solution)/shard_map/all_gather | solution.py:121
  68.4 14.2 %collective-permute-start.4 = (bf16[2048,640]{0,1:T(8,128)(2,1)}, bf16[2048,640]{0,1:T(8,128)(2,1)}, u32[]{:S(2)}, u32[]{:S(2)}) collective-permute-start(bf16[2048,640]{0,1:T(8,128)(2,1)} %all-gather.8.cloned.1.call-done), channel_id=1, source_target_pairs={{0,1},{1,0},{2,3},{3,2},{4,5},{5,4},{6,7},{7,6},{8,9},{9,8},{10,11... | collective-permute-start | bytes 7864328 | tf_op jit(solution)/shard_map/ppermute | solution.py:32
  74.1 15.1 %collective-permute-start.2 = (bf16[128,2048]{1,0:T(8,128)(2,1)}, bf16[128,2048]{1,0:T(8,128)(2,1)}, u32[]{:S(2)}, u32[]{:S(2)}) collective-permute-start(bf16[128,2048]{1,0:T(8,128)(2,1)} %fusion.23), channel_id=1, source_target_pairs={{0,2},{2,4},{4,6},{6,0},{1,3},{3,5},{5,7},{7,1},{8,10},{10,12},{12... | collective-permute-start | bytes 1572872 | tf_op jit(solution)/shard_map/ppermute | solution.py:36
  75.3 26.0 %collective-permute-start.1 = (bf16[128,2048]{1,0:T(8,128)(2,1)}, bf16[128,2048]{1,0:T(8,128)(2,1)}, u32[]{:S(2)}, u32[]{:S(2)}) collective-permute-start(bf16[128,2048]{1,0:T(8,128)(2,1)} %fusion.23), channel_id=1, source_target_pairs={{0,4},{2,6},{4,0},{6,2},{1,5},{3,7},{5,1},{7,3},{8,12},{10,14},{12... | collective-permute-start | bytes 1572872 | tf_op jit(solution)/shard_map/ppermute | solution.py:36
  77.7 23.6 %collective-permute-start = (bf16[128,2048]{1,0:T(8,128)(2,1)}, bf16[128,2048]{1,0:T(8,128)(2,1)}, u32[]{:S(2)}, u32[]{:S(2)}) collective-permute-start(bf16[128,2048]{1,0:T(8,128)(2,1)} %fusion.23), channel_id=1, source_target_pairs={{0,6},{2,0},{4,2},{6,4},{1,7},{3,1},{5,3},{7,5},{8,14},{10,8},{12,... | collective-permute-start | bytes 1572872 | tf_op jit(solution)/shard_map/ppermute | solution.py:36
  81.2 434.2 %reduce-scatter.7.cloned.1.call-start = ((), (), s32[]{:S(2)}) async-start(), calls=%async_computation.9 | async-start | bytes 3244032 | tf_op jit(solution)/shard_map/reduce_scatter | solution.py:213
  106.8 13.6 %collective-permute-start.5 = (bf16[512,256]{1,0:T(8,128)(2,1)S(1)}, bf16[512,256]{1,0:T(8,128)(2,1)S(1)}, u32[]{:S(2)}, u32[]{:S(2)}) collective-permute-start(bf16[512,256]{1,0:T(8,128)(2,1)S(1)} %pad_maximum_fusion.29), channel_id=1, source_target_pairs={{0,8},{8,0},{1,9},{9,1},{2,10},{10,2},{3,11},{11,3},{4,12},{12,4},... | collective-permute-start | bytes 786440 | tf_op jit(solution)/shard_map/ppermute | solution.py:156
  121.3 16.1 %collective-permute-start.6 = (bf16[1024,256]{1,0:T(8,128)(2,1)}, bf16[1024,256]{1,0:T(8,128)(2,1)}, u32[]{:S(2)}, u32[]{:S(2)}) collective-permute-start(bf16[1024,256]{1,0:T(8,128)(2,1)} %pad_maximum_fusion.19), channel_id=1, source_target_pairs={{0,1},{1,0},{2,3},{3,2},{4,5},{5,4},{6,7},{7,6},{8,9},{9,8},{10,11... | collective-permute-start | bytes 1572872 | tf_op jit(solution)/shard_map/ppermute | solution.py:32
  126.8 129.6 %collective-permute-start.15 = (bf16[2048,704]{0,1:T(8,128)(2,1)}, bf16[2048,704]{0,1:T(8,128)(2,1)}, u32[]{:S(2)}, u32[]{:S(2)}) collective-permute-start(bf16[2048,704]{0,1:T(8,128)(2,1)} %all-gather.14.cloned.1.call-done), channel_id=1, source_target_pairs={{0,1},{1,0},{2,3},{3,2},{4,5},{5,4},{6,7},{7,6},{8,9},{9,8},{10,11... | collective-permute-start | bytes 8650760 | tf_op jit(solution)/shard_map/ppermute | solution.py:32
  158.3 28.5 %collective-permute-start.9 = (bf16[128,2048]{1,0:T(8,128)(2,1)}, bf16[128,2048]{1,0:T(8,128)(2,1)S(1)}, u32[]{:S(2)}, u32[]{:S(2)}) collective-permute-start(bf16[128,2048]{1,0:T(8,128)(2,1)} %get-tuple-element.91), channel_id=1, source_target_pairs={{0,6},{2,0},{4,2},{6,4},{1,7},{3,1},{5,3},{7,5},{8,14},{10,8},{12,... | collective-permute-start | bytes 1572872 | tf_op jit(solution)/shard_map/ppermute | solution.py:36
  160.4 27.6 %collective-permute-start.8 = (bf16[128,2048]{1,0:T(8,128)(2,1)}, bf16[128,2048]{1,0:T(8,128)(2,1)}, u32[]{:S(2)}, u32[]{:S(2)}) collective-permute-start(bf16[128,2048]{1,0:T(8,128)(2,1)} %get-tuple-element.92), channel_id=1, source_target_pairs={{0,2},{2,4},{4,6},{6,0},{1,3},{3,5},{5,7},{7,1},{8,10},{10,12},{12... | collective-permute-start | bytes 1572872 | tf_op jit(solution)/shard_map/ppermute | solution.py:36
  160.4 72.5 %collective-permute-start.7 = (bf16[128,2048]{1,0:T(8,128)(2,1)}, bf16[128,2048]{1,0:T(8,128)(2,1)}, u32[]{:S(2)}, u32[]{:S(2)}) collective-permute-start(bf16[128,2048]{1,0:T(8,128)(2,1)} %get-tuple-element.90), channel_id=1, source_target_pairs={{0,4},{2,6},{4,0},{6,2},{1,5},{3,7},{5,1},{7,3},{8,12},{10,14},{12... | collective-permute-start | bytes 1572872 | tf_op jit(solution)/shard_map/ppermute | solution.py:36
  179.9 104.0 %collective-permute-start.14 = (bf16[2048,704]{0,1:T(8,128)(2,1)}, bf16[2048,704]{0,1:T(8,128)(2,1)}, u32[]{:S(2)}, u32[]{:S(2)}) collective-permute-start(bf16[2048,704]{0,1:T(8,128)(2,1)} %all-gather.12.cloned.1.call-done), channel_id=1, source_target_pairs={{0,1},{1,0},{2,3},{3,2},{4,5},{5,4},{6,7},{7,6},{8,9},{9,8},{10,11... | collective-permute-start | bytes 8650760 | tf_op jit(solution)/shard_map/ppermute | solution.py:32
  186.9 53.1 %collective-permute-start.22 = (bf16[128,2048]{1,0:T(8,128)(2,1)}, bf16[128,2048]{1,0:T(8,128)(2,1)}, u32[]{:S(2)}, u32[]{:S(2)}) collective-permute-start(bf16[128,2048]{1,0:T(8,128)(2,1)} %fusion.20), channel_id=1, source_target_pairs={{0,2},{2,4},{4,6},{6,0},{1,3},{3,5},{5,7},{7,1},{8,10},{10,12},{12... | collective-permute-start | bytes 1572872 | tf_op jit(solution)/shard_map/ppermute | solution.py:36
  187.9 54.7 %collective-permute-start.21 = (bf16[128,2048]{1,0:T(8,128)(2,1)}, bf16[128,2048]{1,0:T(8,128)(2,1)}, u32[]{:S(2)}, u32[]{:S(2)}) collective-permute-start(bf16[128,2048]{1,0:T(8,128)(2,1)} %fusion.20), channel_id=1, source_target_pairs={{0,4},{2,6},{4,0},{6,2},{1,5},{3,7},{5,1},{7,3},{8,12},{10,14},{12... | collective-permute-start | bytes 1572872 | tf_op jit(solution)/shard_map/ppermute | solution.py:36
  232.8 54.6 %collective-permute-start.13 = (bf16[2048,704]{0,1:T(8,128)(2,1)}, bf16[2048,704]{0,1:T(8,128)(2,1)S(1)}, u32[]{:S(2)}, u32[]{:S(2)}) collective-permute-start(bf16[2048,704]{0,1:T(8,128)(2,1)} %all-gather.10.cloned.1.call-done), channel_id=1, source_target_pairs={{0,1},{1,0},{2,3},{3,2},{4,5},{5,4},{6,7},{7,6},{8,9},{9,8},{10,11... | collective-permute-start | bytes 8650760 | tf_op jit(solution)/shard_map/ppermute | solution.py:32
  240.0 14.1 %collective-permute-start.20 = (bf16[128,2048]{1,0:T(8,128)(2,1)}, bf16[128,2048]{1,0:T(8,128)(2,1)S(1)}, u32[]{:S(2)}, u32[]{:S(2)}) collective-permute-start(bf16[128,2048]{1,0:T(8,128)(2,1)} %fusion.20), channel_id=1, source_target_pairs={{0,6},{2,0},{4,2},{6,4},{1,7},{3,1},{5,3},{7,5},{8,14},{10,8},{12,... | collective-permute-start | bytes 1572872 | tf_op jit(solution)/shard_map/ppermute | solution.py:36
  242.7 18.8 %collective-permute-start.12 = (bf16[128,2048]{1,0:T(8,128)(2,1)S(1)}, bf16[128,2048]{1,0:T(8,128)(2,1)S(1)}, u32[]{:S(2)}, u32[]{:S(2)}) collective-permute-start(bf16[128,2048]{1,0:T(8,128)(2,1)S(1)} %multiply_convert_fusion.8), channel_id=1, source_target_pairs={{0,2},{2,4},{4,6},{6,0},{1,3},{3,5},{5,7},{7,1},{8,10},{10,12},{12... | collective-permute-start | bytes 1572872 | tf_op jit(solution)/shard_map/ppermute | solution.py:36
  254.1 14.1 %collective-permute-start.11 = (bf16[128,2048]{1,0:T(8,128)(2,1)S(1)}, bf16[128,2048]{1,0:T(8,128)(2,1)S(1)}, u32[]{:S(2)}, u32[]{:S(2)}) collective-permute-start(bf16[128,2048]{1,0:T(8,128)(2,1)S(1)} %multiply_convert_fusion.8), channel_id=1, source_target_pairs={{0,4},{2,6},{4,0},{6,2},{1,5},{3,7},{5,1},{7,3},{8,12},{10,14},{12... | collective-permute-start | bytes 1572872 | tf_op jit(solution)/shard_map/ppermute | solution.py:36
  256.5 24.0 %collective-permute-start.10 = (bf16[128,2048]{1,0:T(8,128)(2,1)S(1)}, bf16[128,2048]{1,0:T(8,128)(2,1)S(1)}, u32[]{:S(2)}, u32[]{:S(2)}) collective-permute-start(bf16[128,2048]{1,0:T(8,128)(2,1)S(1)} %multiply_convert_fusion.8), channel_id=1, source_target_pairs={{0,6},{2,0},{4,2},{6,4},{1,7},{3,1},{5,3},{7,5},{8,14},{10,8},{12,... | collective-permute-start | bytes 1572872 | tf_op jit(solution)/shard_map/ppermute | solution.py:36
  305.2 22.9 %collective-permute-start.25 = (bf16[128,2048]{1,0:T(8,128)(2,1)S(1)}, bf16[128,2048]{1,0:T(8,128)(2,1)S(1)}, u32[]{:S(2)}, u32[]{:S(2)}) collective-permute-start(bf16[128,2048]{1,0:T(8,128)(2,1)S(1)} %get-tuple-element.85), channel_id=1, source_target_pairs={{0,6},{2,0},{4,2},{6,4},{1,7},{3,1},{5,3},{7,5},{8,14},{10,8},{12,... | collective-permute-start | bytes 1572872 | tf_op jit(solution)/shard_map/ppermute | solution.py:36
  308.3 19.8 %collective-permute-start.24 = (bf16[128,2048]{1,0:T(8,128)(2,1)S(1)}, bf16[128,2048]{1,0:T(8,128)(2,1)S(1)}, u32[]{:S(2)}, u32[]{:S(2)}) collective-permute-start(bf16[128,2048]{1,0:T(8,128)(2,1)S(1)} %get-tuple-element.86), channel_id=1, source_target_pairs={{0,2},{2,4},{4,6},{6,0},{1,3},{3,5},{5,7},{7,1},{8,10},{10,12},{12... | collective-permute-start | bytes 1572872 | tf_op jit(solution)/shard_map/ppermute | solution.py:36
  308.3 23.8 %collective-permute-start.23 = (bf16[128,2048]{1,0:T(8,128)(2,1)S(1)}, bf16[128,2048]{1,0:T(8,128)(2,1)S(1)}, u32[]{:S(2)}, u32[]{:S(2)}) collective-permute-start(bf16[128,2048]{1,0:T(8,128)(2,1)S(1)} %get-tuple-element.84), channel_id=1, source_target_pairs={{0,4},{2,6},{4,0},{6,2},{1,5},{3,7},{5,1},{7,3},{8,12},{10,14},{12... | collective-permute-start | bytes 1572872 | tf_op jit(solution)/shard_map/ppermute | solution.py:36
  315.6 36.8 %collective-permute-start.18 = (bf16[128,2048]{1,0:T(8,128)(2,1)S(1)}, bf16[128,2048]{1,0:T(8,128)(2,1)S(1)}, u32[]{:S(2)}, u32[]{:S(2)}) collective-permute-start(bf16[128,2048]{1,0:T(8,128)(2,1)S(1)} %get-tuple-element.88), channel_id=1, source_target_pairs={{0,6},{2,0},{4,2},{6,4},{1,7},{3,1},{5,3},{7,5},{8,14},{10,8},{12,... | collective-permute-start | bytes 1572872 | tf_op jit(solution)/shard_map/ppermute | solution.py:36
  317.2 35.3 %collective-permute-start.17 = (bf16[128,2048]{1,0:T(8,128)(2,1)S(1)}, bf16[128,2048]{1,0:T(8,128)(2,1)S(1)}, u32[]{:S(2)}, u32[]{:S(2)}) collective-permute-start(bf16[128,2048]{1,0:T(8,128)(2,1)S(1)} %get-tuple-element.89), channel_id=1, source_target_pairs={{0,2},{2,4},{4,6},{6,0},{1,3},{3,5},{5,7},{7,1},{8,10},{10,12},{12... | collective-permute-start | bytes 1572872 | tf_op jit(solution)/shard_map/ppermute | solution.py:36
  328.1 26.6 %collective-permute-start.16 = (bf16[128,2048]{1,0:T(8,128)(2,1)S(1)}, bf16[128,2048]{1,0:T(8,128)(2,1)S(1)}, u32[]{:S(2)}, u32[]{:S(2)}) collective-permute-start(bf16[128,2048]{1,0:T(8,128)(2,1)S(1)} %get-tuple-element.87), channel_id=1, source_target_pairs={{0,4},{2,6},{4,0},{6,2},{1,5},{3,7},{5,1},{7,3},{8,12},{10,14},{12... | collective-permute-start | bytes 1572872 | tf_op jit(solution)/shard_map/ppermute | solution.py:36
  356.6 11.7 %collective-permute-start.28 = (bf16[128,2048]{1,0:T(8,128)(2,1)S(1)}, bf16[128,2048]{1,0:T(8,128)(2,1)S(1)}, u32[]{:S(2)}, u32[]{:S(2)}) collective-permute-start(bf16[128,2048]{1,0:T(8,128)(2,1)S(1)} %get-tuple-element.46), channel_id=1, source_target_pairs={{0,2},{2,4},{4,6},{6,0},{1,3},{3,5},{5,7},{7,1},{8,10},{10,12},{12... | collective-permute-start | bytes 1572872 | tf_op jit(solution)/shard_map/ppermute | solution.py:36
  356.6 24.2 %collective-permute-start.27 = (bf16[128,2048]{1,0:T(8,128)(2,1)S(1)}, bf16[128,2048]{1,0:T(8,128)(2,1)S(1)}, u32[]{:S(2)}, u32[]{:S(2)}) collective-permute-start(bf16[128,2048]{1,0:T(8,128)(2,1)S(1)} %get-tuple-element.46), channel_id=1, source_target_pairs={{0,4},{2,6},{4,0},{6,2},{1,5},{3,7},{5,1},{7,3},{8,12},{10,14},{12... | collective-permute-start | bytes 1572872 | tf_op jit(solution)/shard_map/ppermute | solution.py:36
  359.2 23.3 %collective-permute-start.26 = (bf16[128,2048]{1,0:T(8,128)(2,1)S(1)}, bf16[128,2048]{1,0:T(8,128)(2,1)S(1)}, u32[]{:S(2)}, u32[]{:S(2)}) collective-permute-start(bf16[128,2048]{1,0:T(8,128)(2,1)S(1)} %get-tuple-element.46), channel_id=1, source_target_pairs={{0,6},{2,0},{4,2},{6,4},{1,7},{3,1},{5,3},{7,5},{8,14},{10,8},{12,... | collective-permute-start | bytes 1572872 | tf_op jit(solution)/shard_map/ppermute | solution.py:36
  363.8 50.4 %collective-permute-start.41 = (bf16[2048,704]{0,1:T(8,128)(2,1)}, bf16[2048,704]{0,1:T(8,128)(2,1)S(1)}, u32[]{:S(2)}, u32[]{:S(2)}) collective-permute-start(bf16[2048,704]{0,1:T(8,128)(2,1)} %convolution_convert_fusion.2), channel_id=1, source_target_pairs={{0,1},{1,0},{2,3},{3,2},{4,5},{5,4},{6,7},{7,6},{8,9},{9,8},{10,11... | collective-permute-start | bytes 8650760 | tf_op jit(solution)/shard_map/ppermute | solution.py:32
  411.7 5.5 collective-permute-start.29
  417.2 247.7 %all-gather.16.cloned.1.call-start = ((), (), s32[]{:S(2)}) async-start(), calls=%async_computation.12 | async-start | bytes 2113536 | tf_op jit(solution)/shard_map/all_gather | solution.py:265
  419.4 11.2 %collective-permute-start.30 = (bf16[512,256]{1,0:T(8,128)(2,1)S(1)}, bf16[512,256]{1,0:T(8,128)(2,1)S(1)}, u32[]{:S(2)}, u32[]{:S(2)}) collective-permute-start(bf16[512,256]{1,0:T(8,128)(2,1)S(1)} %slice.636), channel_id=1, source_target_pairs={{0,8},{8,0},{1,9},{9,1},{2,10},{10,2},{3,11},{11,3},{4,12},{12,4},... | collective-permute-start | bytes 786440 | tf_op jit(solution)/shard_map/ppermute | solution.py:156
  435.6 12.0 %collective-permute-start.33 = (bf16[128,2048]{1,0:T(8,128)(2,1)S(1)}, bf16[128,2048]{1,0:T(8,128)(2,1)S(1)}, u32[]{:S(2)}, u32[]{:S(2)}) collective-permute-start(bf16[128,2048]{1,0:T(8,128)(2,1)S(1)} %get-tuple-element.80), channel_id=1, source_target_pairs={{0,6},{2,0},{4,2},{6,4},{1,7},{3,1},{5,3},{7,5},{8,14},{10,8},{12,... | collective-permute-start | bytes 1572872 | tf_op jit(solution)/shard_map/ppermute | solution.py:36
  437.7 13.8 %collective-permute-start.32 = (bf16[128,2048]{1,0:T(8,128)(2,1)S(1)}, bf16[128,2048]{1,0:T(8,128)(2,1)S(1)}, u32[]{:S(2)}, u32[]{:S(2)}) collective-permute-start(bf16[128,2048]{1,0:T(8,128)(2,1)S(1)} %get-tuple-element.81), channel_id=1, source_target_pairs={{0,2},{2,4},{4,6},{6,0},{1,3},{3,5},{5,7},{7,1},{8,10},{10,12},{12... | collective-permute-start | bytes 1572872 | tf_op jit(solution)/shard_map/ppermute | solution.py:36
  437.7 22.9 %collective-permute-start.31 = (bf16[128,2048]{1,0:T(8,128)(2,1)S(1)}, bf16[128,2048]{1,0:T(8,128)(2,1)S(1)}, u32[]{:S(2)}, u32[]{:S(2)}) collective-permute-start(bf16[128,2048]{1,0:T(8,128)(2,1)S(1)} %get-tuple-element.79), channel_id=1, source_target_pairs={{0,4},{2,6},{4,0},{6,2},{1,5},{3,7},{5,1},{7,3},{8,12},{10,14},{12... | collective-permute-start | bytes 1572872 | tf_op jit(solution)/shard_map/ppermute | solution.py:36
  462.6 246.6 %reduce-scatter.9.cloned.1.call-start = ((), (), s32[]{:S(2)}) async-start(), calls=%async_computation.10 | async-start | bytes 3244032 | tf_op jit(solution)/shard_map/reduce_scatter | solution.py:213
  465.5 8.9 %collective-permute-start.46 = (bf16[2048,704]{0,1:T(8,128)(2,1)S(1)}, bf16[2048,704]{0,1:T(8,128)(2,1)S(1)}, u32[]{:S(2)}, u32[]{:S(2)}) collective-permute-start(bf16[2048,704]{0,1:T(8,128)(2,1)S(1)} %convolution_convert_fusion.1), channel_id=1, source_target_pairs={{0,1},{1,0},{2,3},{3,2},{4,5},{5,4},{6,7},{7,6},{8,9},{9,8},{10,11... | collective-permute-start | bytes 8650760 | tf_op jit(solution)/shard_map/ppermute | solution.py:32
  477.4 279.3 %reduce-scatter.11.cloned.1.call-start = ((), (), s32[]{:S(2)}) async-start(), calls=%async_computation.11 | async-start | bytes 3244032 | tf_op jit(solution)/shard_map/reduce_scatter | solution.py:213
  481.7 5.6 collective-permute-start.51
  492.0 310.7 %reduce-scatter.5.cloned.1.call-start = ((), (), s32[]{:S(2)}) async-start(), calls=%async_computation.8 | async-start | bytes 2949120 | tf_op jit(solution)/shard_map/reduce_scatter | solution.py:213
  504.2 7.0 collective-permute-start.35
  504.6 4.2 collective-permute-start.19
  515.4 241.9 %collective-permute-start.42 = (bf16[256,704]{0,1:T(8,128)(2,1)}, bf16[256,704]{0,1:T(8,128)(2,1)S(1)}, u32[]{:S(2)}, u32[]{:S(2)}) collective-permute-start(bf16[256,704]{0,1:T(8,128)(2,1)} %reduce-scatter.7.cloned.1.call-done), channel_id=1, source_target_pairs={{0,8},{8,0},{1,9},{9,1},{2,10},{10,2},{3,11},{11,3},{4,12},{12,4},... | collective-permute-start | bytes 1081352 | tf_op jit(solution)/shard_map/ppermute | solution.py:156
  709.1 51.8 %collective-permute-start.47 = (bf16[256,704]{0,1:T(8,128)(2,1)}, bf16[256,704]{0,1:T(8,128)(2,1)S(1)}, u32[]{:S(2)}, u32[]{:S(2)}) collective-permute-start(bf16[256,704]{0,1:T(8,128)(2,1)} %reduce-scatter.9.cloned.1.call-done), channel_id=1, source_target_pairs={{0,8},{8,0},{1,9},{9,1},{2,10},{10,2},{3,11},{11,3},{4,12},{12,4},... | collective-permute-start | bytes 1081352 | tf_op jit(solution)/shard_map/ppermute | solution.py:156
  756.7 8.0 collective-permute-start.52
  757.4 11.0 %collective-permute-start.43 = (bf16[256,704]{0,1:T(8,128)(2,1)S(1)}, bf16[256,704]{0,1:T(8,128)(2,1)S(1)}, u32[]{:S(2)}, u32[]{:S(2)}) collective-permute-start(bf16[256,704]{0,1:T(8,128)(2,1)S(1)} %get-tuple-element.42), channel_id=1, source_target_pairs={{0,6},{2,0},{4,2},{6,4},{1,7},{3,1},{5,3},{7,5},{8,14},{10,8},{12,... | collective-permute-start | bytes 1081352 | tf_op jit(solution)/shard_map/ppermute | solution.py:36
  759.9 8.9 %collective-permute-start.44 = (bf16[256,704]{0,1:T(8,128)(2,1)S(1)}, bf16[256,704]{0,1:T(8,128)(2,1)S(1)}, u32[]{:S(2)}, u32[]{:S(2)}) collective-permute-start(bf16[256,704]{0,1:T(8,128)(2,1)S(1)} %get-tuple-element.42), channel_id=1, source_target_pairs={{0,4},{2,6},{4,0},{6,2},{1,5},{3,7},{5,1},{7,3},{8,12},{10,14},{12... | collective-permute-start | bytes 1081352 | tf_op jit(solution)/shard_map/ppermute | solution.py:36
  760.4 20.7 %collective-permute-start.45 = (bf16[256,704]{0,1:T(8,128)(2,1)S(1)}, bf16[256,704]{0,1:T(8,128)(2,1)S(1)}, u32[]{:S(2)}, u32[]{:S(2)}) collective-permute-start(bf16[256,704]{0,1:T(8,128)(2,1)S(1)} %get-tuple-element.42), channel_id=1, source_target_pairs={{0,2},{2,4},{4,6},{6,0},{1,3},{3,5},{5,7},{7,1},{8,10},{10,12},{12... | collective-permute-start | bytes 1081352 | tf_op jit(solution)/shard_map/ppermute | solution.py:36
  762.1 21.7 %collective-permute-start.48 = (bf16[256,704]{0,1:T(8,128)(2,1)S(1)}, bf16[256,704]{0,1:T(8,128)(2,1)S(1)}, u32[]{:S(2)}, u32[]{:S(2)}) collective-permute-start(bf16[256,704]{0,1:T(8,128)(2,1)S(1)} %get-tuple-element.40), channel_id=1, source_target_pairs={{0,6},{2,0},{4,2},{6,4},{1,7},{3,1},{5,3},{7,5},{8,14},{10,8},{12,... | collective-permute-start | bytes 1081352 | tf_op jit(solution)/shard_map/ppermute | solution.py:36
  764.7 19.2 %collective-permute-start.49 = (bf16[256,704]{0,1:T(8,128)(2,1)S(1)}, bf16[256,704]{0,1:T(8,128)(2,1)S(1)}, u32[]{:S(2)}, u32[]{:S(2)}) collective-permute-start(bf16[256,704]{0,1:T(8,128)(2,1)S(1)} %get-tuple-element.40), channel_id=1, source_target_pairs={{0,4},{2,6},{4,0},{6,2},{1,5},{3,7},{5,1},{7,3},{8,12},{10,14},{12... | collective-permute-start | bytes 1081352 | tf_op jit(solution)/shard_map/ppermute | solution.py:36
  768.4 27.1 %collective-permute-start.50 = (bf16[256,704]{0,1:T(8,128)(2,1)S(1)}, bf16[256,704]{0,1:T(8,128)(2,1)S(1)}, u32[]{:S(2)}, u32[]{:S(2)}) collective-permute-start(bf16[256,704]{0,1:T(8,128)(2,1)S(1)} %get-tuple-element.40), channel_id=1, source_target_pairs={{0,2},{2,4},{4,6},{6,0},{1,3},{3,5},{5,7},{7,1},{8,10},{10,12},{12... | collective-permute-start | bytes 1081352 | tf_op jit(solution)/shard_map/ppermute | solution.py:36
  768.8 30.5 %collective-permute-start.53 = (bf16[256,704]{0,1:T(8,128)(2,1)}, bf16[256,704]{0,1:T(8,128)(2,1)S(1)}, u32[]{:S(2)}, u32[]{:S(2)}) collective-permute-start(bf16[256,704]{0,1:T(8,128)(2,1)} %get-tuple-element.38), channel_id=1, source_target_pairs={{0,6},{2,0},{4,2},{6,4},{1,7},{3,1},{5,3},{7,5},{8,14},{10,8},{12,... | collective-permute-start | bytes 1081352 | tf_op jit(solution)/shard_map/ppermute | solution.py:36
  781.1 22.3 %collective-permute-start.54 = (bf16[256,704]{0,1:T(8,128)(2,1)}, bf16[256,704]{0,1:T(8,128)(2,1)S(1)}, u32[]{:S(2)}, u32[]{:S(2)}) collective-permute-start(bf16[256,704]{0,1:T(8,128)(2,1)} %get-tuple-element.38), channel_id=1, source_target_pairs={{0,4},{2,6},{4,0},{6,2},{1,5},{3,7},{5,1},{7,3},{8,12},{10,14},{12... | collective-permute-start | bytes 1081352 | tf_op jit(solution)/shard_map/ppermute | solution.py:36
  783.8 24.1 %collective-permute-start.55 = (bf16[256,704]{0,1:T(8,128)(2,1)}, bf16[256,704]{0,1:T(8,128)(2,1)}, u32[]{:S(2)}, u32[]{:S(2)}) collective-permute-start(bf16[256,704]{0,1:T(8,128)(2,1)} %get-tuple-element.38), channel_id=1, source_target_pairs={{0,2},{2,4},{4,6},{6,0},{1,3},{3,5},{5,7},{7,1},{8,10},{10,12},{12... | collective-permute-start | bytes 1081352 | tf_op jit(solution)/shard_map/ppermute | solution.py:36
  802.7 7.9 collective-permute-start.36
  811.7 9.7 %collective-permute-start.37 = (bf16[256,640]{0,1:T(8,128)(2,1)S(1)}, bf16[256,640]{0,1:T(8,128)(2,1)S(1)}, u32[]{:S(2)}, u32[]{:S(2)}) collective-permute-start(bf16[256,640]{0,1:T(8,128)(2,1)S(1)} %get-tuple-element.44), channel_id=1, source_target_pairs={{0,6},{2,0},{4,2},{6,4},{1,7},{3,1},{5,3},{7,5},{8,14},{10,8},{12,... | collective-permute-start | bytes 983048 | tf_op jit(solution)/shard_map/ppermute | solution.py:36
  815.5 7.5 collective-permute-start.38
  816.9 9.5 %collective-permute-start.39 = (bf16[256,640]{0,1:T(8,128)(2,1)S(1)}, bf16[256,640]{0,1:T(8,128)(2,1)S(1)}, u32[]{:S(2)}, u32[]{:S(2)}) collective-permute-start(bf16[256,640]{0,1:T(8,128)(2,1)S(1)} %get-tuple-element.44), channel_id=1, source_target_pairs={{0,2},{2,4},{4,6},{6,0},{1,3},{3,5},{5,7},{7,1},{8,10},{10,12},{12... | collective-permute-start | bytes 983048 | tf_op jit(solution)/shard_map/ppermute | solution.py:36
  828.9 19.9 %collective-permute-start.40 = (bf16[2,256,640]{1,2,0:T(8,128)(2,1)}, bf16[2,256,640]{1,2,0:T(8,128)(2,1)}, u32[]{:S(2)}, u32[]{:S(2)}) collective-permute-start(bf16[2,256,640]{1,2,0:T(8,128)(2,1)} %constant_dynamic-slice_fusion.1), channel_id=1, source_target_pairs={{0,1},{1,0},{2,3},{3,2},{4,5},{5,4},{6,7},{7,6},{8,9},{9,8},{10,11... | collective-permute-start | bytes 1966088 | tf_op jit(solution)/shard_map/ppermute | solution.py:32
  (93 other events, 1567.3 us)
Sparse Core Ops, SparseCore 0:
  21.6 46.7 all-gather.7
  70.6 56.2 all-gather.13
  128.4 51.4 all-gather.11
  181.4 51.4 all-gather.9
  417.3 41.7 reduce-scatter.6
  462.7 202.1 all-gather.15
  667.9 41.1 reduce-scatter.8
  712.1 44.5 reduce-scatter.10
  759.2 43.4 reduce-scatter.4
